TPU v7x, 32 devices: a whole 2x2x4 slice. The times are simulated.
32 devices in a mesh: case: 2 (over x), span: 8 (over z, y), dom: 2 (over core).
Axes of the slice: x: 2, y: 2, z: 4, core: 2. Of those that a mesh axis runs over, the one named last changes fastest.
Arguments:
- scalar: float32 [256, 8192], P(('case', 'span'), 'dom'), parts along dimension 0, may hold values from -6 to 6
- span_vel: float32 [256, 8192], P(('case', 'span'), 'dom'), parts along dimension 0, may hold values from -4 to 4
- flux_weight: float32 [4, 8192], P(None, 'dom'), may hold values from -4 to 4
- neighbours: int32 [4, 8192], P(None, 'dom'), may hold values from 0 to 8191, as said below
- diagonal: float32 [8192], P('dom'), may hold values from 0.5 to 2
- interface: int32 [16, 128], P('dom'), may hold values from 0 to 8191, as said below
- schur_one: float32 [128, 8, 128, 128], P('span', 'dom'), may hold values from -1 to 1
- schur_two: float32 [128, 4, 128, 128], P('span', 'dom'), may hold values from -1 to 1
- schur_three: float32 [128, 2, 128, 128], P('span', 'dom'), may hold values from -1 to 1
- schur_root: float32 [128, 1, 128, 128], P('span'), may hold values from -1 to 1
Outputs:
- pressure: float32 [256, 8192], P(('case', 'span'), 'dom'), parts along dimension 0
- corrected: float32 [256, 8192], P(('case', 'span'), 'dom'), parts along dimension 0
There are 2 independent parts, one for each index of `case`. A program takes and returns all parts, laid end to end along the dimension named above; an argument that names none is the same for every part. Nothing has to cross between parts.
Inputs may be any that keep to these rules, and one draw needn't show every extreme that they name: `neighbours`: every entry lies 1 to 64 cells from its own cell in the numbering, and the distance 64 occurs. `interface`: row d holds 128 distinct cells of subdomain d, numbered from d * 512 to (d + 1) * 512 - 1.
All inputs are finite; a program needn't handle non-finite values.
Results may differ from a plain program's by a relative error of at most 0.0001.
Values sent between devices are 32-bit elements; how exact they have to be, the bound alone decides.
No kernel may reach another device: no remote copies, remote signals or barrier semaphores. Data moves between devices by JAX's collectives and lax.ppermute only.
A program may use at most 64 MiB of HBM per device.

v0:
```python
import functools
import math

import jax
import jax.numpy as jnp
from jax import lax
from jax.experimental import pallas as pl
from jax.experimental.pallas import tpu as pltpu
from jax.sharding import PartitionSpec as P


PLANES = 128
LANES = 128
SUB = 8
HALF = LANES // 2
F32 = jnp.float32
EXACT = lax.Precision.HIGHEST


def fourier_entry(wave_ids, plane_ids):
    middle = PLANES // 2
    wave_num = jnp.where(wave_ids <= middle, wave_ids, wave_ids - middle)
    phase_angle = (wave_num * plane_ids % PLANES).astype(F32) * (2.0 * math.pi / PLANES)
    at_edge = (wave_ids == 0) | (wave_ids == middle)
    weight_row = jnp.where(at_edge, math.sqrt(1.0 / PLANES), math.sqrt(2.0 / PLANES))
    return jnp.where(wave_ids <= middle, jnp.cos(phase_angle), jnp.sin(phase_angle)) * weight_row


def wave_shift(wave_ids):
    middle = PLANES // 2
    wave_num = jnp.where(wave_ids <= middle, wave_ids, wave_ids - middle).astype(F32)
    return (2.0 * jnp.sin(wave_num * (math.pi / PLANES))) ** 2


def xor_permute(value, axis, mask):
    return lax.ppermute(value, axis, [(i, i ^ mask) for i in range(lax.axis_size(axis))])


def gathered(block, axis):
    count = lax.axis_size(axis)
    far = [xor_permute(block, axis, mask) for mask in range(count - 2, 0, -2)]
    mine = jnp.concatenate([block] + far[::-1], axis=0)
    return mine, xor_permute(mine, axis, 1)


def xor_offsets(count):
    return list(range(0, count, 2)) + list(range(1, count, 2))


def whole(*shapes):
    return [pl.BlockSpec(memory_space=pltpu.VMEM) for _ in shapes]


def lane_take(source, index):
    return jnp.take_along_axis(source, index, axis=1, mode="promise_in_bounds")


def decay(diag):
    root = jnp.sqrt(diag + 0.25 * diag * diag)
    return 1.0 / (1.0 + 0.5 * diag + root), 0.5 / root


def powers(base, exponent, limit):
    result = None
    bit, factor = 1, base
    while bit < limit:
        part = jnp.where((exponent & bit) != 0, factor, 1.0)
        result = part if result is None else result * part
        factor = factor * factor
        bit *= 2
    return result


def convection(ext, block, nblocks, rows, sv, fw_ref, nb_ref):
    start = pl.multiple_of(block * LANES, LANES)
    here = pl.multiple_of(start + LANES, LANES)
    field = ext[pl.ds(SUB, rows), pl.ds(here, LANES)]
    before = ext[pl.ds(SUB, rows), pl.ds(start, LANES)]
    after = ext[pl.ds(SUB, rows), pl.ds(pl.multiple_of(here + LANES, LANES), LANES)]
    lane = lax.broadcasted_iota(jnp.int32, (rows, LANES), 1)
    around = jnp.where(lane < HALF, after, before)
    ahead = ext[pl.ds(SUB + 1, rows), pl.ds(here, LANES)]
    behind = ext[pl.ds(SUB - 1, rows), pl.ds(here, LANES)]
    total = sv * 0.5 * (ahead - behind)
    for slot in range(fw_ref.shape[0]):
        ids = nb_ref[pl.ds(slot, 1), pl.ds(start, LANES)]
        index = jnp.broadcast_to(ids & (LANES - 1), (rows, LANES))
        inside = (((ids >> 7) - block) & (nblocks - 1)) == 0
        near = jnp.where(inside, lane_take(field, index), lane_take(around, index))
        total = total + fw_ref[pl.ds(slot, 1), pl.ds(start, LANES)] * (near - field)
    return field, total


def fill(ext, field_ref, halo_ref, rows, cells):
    ext[pl.ds(SUB, rows), pl.ds(LANES, cells)] = field_ref[...]
    ext[pl.ds(SUB, rows), pl.ds(0, LANES)] = halo_ref[...]
    ext[pl.ds(SUB, rows), pl.ds(LANES + cells, LANES)] = halo_ref[...]


def source_kernel(
    planes, halo_ref, v_hbm, sv_hbm, fw_hbm, nb_hbm, diag_hbm, iface_hbm,
    pay_ref, q_ref, edge_ref, dif_ref, v_ref, sv_ref, fw_ref, nb_ref, diag_ref, iface_ref, ext, strip, sems,
):
    rows, cells = v_ref.shape
    moved = (
        (v_hbm, v_ref), (sv_hbm, sv_ref), (fw_hbm, fw_ref), (nb_hbm, nb_ref), (diag_hbm, diag_ref), (iface_hbm, iface_ref),
    )
    moves = [pltpu.make_async_copy(src, dst, sems.at[i]) for i, (src, dst) in enumerate(moved)]
    for move in moves:
        move.start()
    for move in moves:
        move.wait()
    nblocks = cells // LANES
    fill(ext, v_ref, halo_ref, rows, cells)
    ext[pl.ds(0, SUB), :] = jnp.zeros((SUB, cells + 2 * LANES), F32)
    ext[pl.ds(SUB + rows, SUB), :] = jnp.zeros((SUB, cells + 2 * LANES), F32)
    row = lax.broadcasted_iota(jnp.int32, (rows, LANES), 0)

    def step(block, carry):
        start = pl.multiple_of(block * LANES, LANES)
        sv = sv_ref[:, pl.ds(start, LANES)]
        field, total = convection(ext, block, nblocks, rows, sv, fw_ref, nb_ref)
        source = field - total
        diag = diag_ref[pl.ds(block, 1), :]
        lam, kappa = decay(diag)
        forward, backward, factor, shift = source, source, lam, 1
        while shift < planes:
            down = jnp.where(row >= shift, pltpu.roll(forward, shift, 0), 0.0)
            up = jnp.where(row < rows - shift, pltpu.roll(backward, rows - shift, 0), 0.0)
            forward = forward + factor * down
            backward = backward + factor * up
            factor, shift = factor * factor, shift * 2
        local = kappa * (forward + (backward - source))
        q_ref[:, pl.ds(start, LANES)] = local
        last = planes - 1
        edges = (
            local[0:1], local[last:planes], field[0:1], field[last:planes], sv[0:1], sv[last:planes], diag,
        )
        for place, value in enumerate(edges):
            strip[pl.ds(place, 1), pl.ds(start, LANES)] = value
            if place < 6:
                edge_ref[place, pl.ds(block, 1), :] = value
        return carry

    lax.fori_loop(0, nblocks, step, 0, unroll=4)
    domains = iface_ref.shape[0]
    width = cells // domains
    for pair in range(domains // 2):
        total = None
        for domain in (2 * pair, 2 * pair + 1):
            where = iface_ref[pl.ds(domain, 1), :] & (width - 1)
            lane, which = where & (LANES - 1), where >> 7
            inner = jnp.zeros((rows, LANES), F32)
            outer = jnp.zeros((SUB, LANES), F32)
            for part in range(width // LANES):
                start = domain * width + part * LANES
                here = which == part
                index = jnp.broadcast_to(lane, (rows, LANES))
                inner = jnp.where(here, lane_take(q_ref[:, pl.ds(start, LANES)], index), inner)
                index = jnp.broadcast_to(lane, (SUB, LANES))
                outer = jnp.where(here, lane_take(strip[:, pl.ds(start, LANES)], index), outer)
            total = inner if total is None else total + inner
            for place in range(6):
                at = 2 * rows + SUB * (place // 2) + domain
                pay_ref[pl.ds(at, 1), pl.ds((place % 2) * LANES, LANES)] = outer[place : place + 1]
            dif_ref[pl.ds(domain, 1), :] = outer[6:7]
        half, column = divmod(pair, domains // 4)
        pay_ref[pl.ds(half * rows, rows), pl.ds(column * LANES, LANES)] = total


def slots_of(iface_ref, inv_ref):
    domains, slots = iface_ref.shape
    per = inv_ref.shape[0] // domains
    columns = jnp.transpose(jnp.concatenate([iface_ref[...].astype(F32)] * (LANES // domains), axis=0))
    lane = lax.broadcasted_iota(jnp.int32, (slots, LANES), 1)
    slot = lax.broadcasted_iota(jnp.int32, (slots, LANES), 0).astype(F32)
    for domain in range(domains):
        own = columns[:, domain : domain + 1].astype(jnp.int32) & (per * LANES - 1)
        own = jnp.broadcast_to(own, (slots, LANES))
        for part in range(per):
            hit = jnp.where(own == lane + part * LANES, slot, -1.0)
            found = jnp.max(hit, axis=0, keepdims=True)
            inv_ref[pl.ds(domain * per + part, 1), :] = found.astype(jnp.int32)


def stage_kernel(
    iface_ref, m1_hbm, m2_hbm, m3_hbm, root_hbm, inv_ref, m1, flipped, m3, root, m2, sems
):
    moved = ((m2_hbm, m2), (m1_hbm, m1), (m3_hbm, m3), (root_hbm, root))
    moves = [pltpu.make_async_copy(src, dst, sems.at[i]) for i, (src, dst) in enumerate(moved)]
    for move in moves:
        move.start()
    slots_of(iface_ref, inv_ref)
    moves[0].wait()

    def flip(wave, carry):
        for node in range(m2.shape[1]):
            flipped[wave, node] = jnp.transpose(m2[wave, node])
        return carry

    lax.fori_loop(0, m2.shape[0], flip, 0, unroll=2)
    for move in moves[1:]:
        move.wait()


def over_lanes(matrix, row):
    return jnp.sum(matrix * row, axis=1, keepdims=True)


def over_rows(matrix, column):
    return jnp.sum(matrix * column, axis=0, keepdims=True)


def up_kernel(
    offsets, rows, me_ref, mine_ref, recv_ref, table_ref, edge_ref, sigma_ref, dif_ref, m1, flipped, m3,
    s3_ref, keep_ref, q, edges, pairs, spectrum, columns,
):
    waves, nodes = m1.shape[:2]
    count = len(offsets)
    me = me_ref[0]
    block_rows = 2 * rows + 3 * SUB
    for place, offset in enumerate(offsets):
        source = mine_ref if place < count // 2 else recv_ref
        base = (place % (count // 2)) * block_rows
        for half in range(2):
            q[pl.ds(place * rows, rows), pl.ds(half * 2 * LANES, 2 * LANES)] = source[
                pl.ds(base + half * rows, rows), :
            ]
        edges[me ^ offset] = source[pl.ds(base + 2 * rows, 3 * SUB), :]
    wide = jnp.dot(table_ref[...], q[...], precision=EXACT, preferred_element_type=F32)
    for node in range(nodes):
        spectrum[node] = wide[:, node * LANES : (node + 1) * LANES]
    dif = dif_ref[...]
    lam, _ = decay(dif)
    first_of = lambda t, place: edges[t, pl.ds(SUB * place, SUB), pl.ds(0, LANES)]
    last_of = lambda t, place: edges[t, pl.ds(SUB * place, SUB), pl.ds(LANES, LANES)]
    residual = []
    for t in range(count):
        prev, succ = (t - 1) % count, (t + 1) % count
        residual.append(last_of(prev, 0) - lam * first_of(t, 0) + 0.5 * first_of(t, 2) * last_of(prev, 1))
        residual.append(first_of(succ, 0) - lam * last_of(t, 0) - 0.5 * last_of(t, 2) * first_of(succ, 1))

    def edge_step(wave, carry):
        total = edge_ref[wave, 0] * residual[0]
        for place in range(1, 2 * count):
            total = total + edge_ref[wave, place] * residual[place]
        leaf = total / (dif + sigma_ref[wave])
        pairs[wave] = leaf + pltpu.roll(leaf, SUB - 1, 0)
        return carry

    lax.fori_loop(0, waves, edge_step, 0, unroll=2)
    columns[...] = jnp.zeros((LANES, LANES), F32)
    lane = lax.broadcasted_iota(jnp.int32, (LANES, LANES), 1)

    def wave_step(wave, carry):
        sums = []
        for node in range(nodes):
            leaf = spectrum[node, pl.ds(wave, 1), :] + pairs[wave, pl.ds(2 * node, 1), :]
            matrix = m1[wave, node]
            first = over_lanes(matrix, leaf)
            keep_ref[wave, pl.ds(node, 1), :] = over_rows(matrix, first)
            sums.append(first)
        total = None
        for node in range(nodes // 2):
            second = over_rows(flipped[wave, node], sums[2 * node] + sums[2 * node + 1])
            keep_ref[wave, pl.ds(nodes + node, 1), :] = second
            total = second if total is None else total + second
        third = over_lanes(m3[wave, 0], total)
        columns[...] = jnp.where(lane == wave, third, columns[...])
        return carry

    lax.fori_loop(0, waves, wave_step, 0, unroll=2)
    s3_ref[...] = jnp.transpose(columns[...])[: s3_ref.shape[0]]


def down_kernel(s3_ref, other_ref, keep_ref, m1, flipped, m3, root, out_ref, lowered):
    waves, nodes = m1.shape[:2]
    lowered[...] = jnp.zeros((LANES, LANES), F32)
    if out_ref.shape[1] > waves:
        out_ref[...] = jnp.zeros(out_ref.shape, F32)

    def root_step(wave, carry):
        own = s3_ref[pl.ds(wave, 1), :]
        top = over_lanes(root[wave, 0], own + other_ref[pl.ds(wave, 1), :])
        lowered[pl.ds(wave, 1), :] = own - over_rows(root[wave, 0], top)
        return carry

    lax.fori_loop(0, waves, root_step, 0, unroll=4)
    lowered[...] = jnp.transpose(lowered[...])
    lane = lax.broadcasted_iota(jnp.int32, (LANES, LANES), 1)

    def wave_step(wave, carry):
        third = jnp.sum(jnp.where(lane == wave, lowered[...], 0.0), axis=1, keepdims=True)
        third = over_rows(m3[wave, 0], third)
        for pair in range(nodes // 2):
            second = over_lanes(flipped[wave, pair], keep_ref[wave, pl.ds(nodes + pair, 1), :] - third)
            for node in (2 * pair, 2 * pair + 1):
                first = keep_ref[wave, pl.ds(node, 1), :] - over_rows(m1[wave, node], second)
                out_ref[node, pl.ds(wave, 1), :] = first
        return carry

    lax.fori_loop(0, waves, wave_step, 0, unroll=2)


def change_of(pairs, count, mine_ref, recv_ref, table_ref, waves):
    nodes = mine_ref.shape[0] * 2 // waves.shape[0]
    wave_rows = waves.shape[0] // count
    for place in range(count):
        source = mine_ref if place < count // 2 else recv_ref
        base = (place % (count // 2)) * nodes * wave_rows
        for at, pair in enumerate(pairs):
            waves[pl.ds(place * wave_rows, wave_rows), pl.ds(at * LANES, LANES)] = source[
                pl.ds(base + pair * wave_rows, wave_rows), :
            ]
    return jnp.dot(table_ref[...], waves[...], precision=EXACT, preferred_element_type=F32)


def pressure_block(planes, block, change, q_ref, inflow_ref, diag_ref, inv_ref):
    rows = q_ref.shape[0]
    start = block * LANES if isinstance(block, int) else pl.multiple_of(block * LANES, LANES)
    row = lax.broadcasted_iota(jnp.int32, (rows, LANES), 0)
    edge_row = lax.broadcasted_iota(jnp.int32, (SUB, LANES), 0)
    lam, _ = decay(diag_ref[pl.ds(block, 1), :])
    left, right, at_first, at_last = (inflow_ref[i, pl.ds(block, 1), :] for i in range(4))
    from_left = at_first + lam * left
    from_right = at_last + lam * right
    local = q_ref[:, pl.ds(start, LANES)]
    value = local + powers(lam, row, planes) * from_left + powers(lam, (planes - 1) - row, planes) * from_right
    span = lam
    for _ in range(int(math.log2(planes))):
        span = span * span
    before = lam * local[0:1] + left + lam * at_first + span * from_right
    after = lam * local[planes - 1 : planes] + right + lam * at_last + span * from_left
    outer = jnp.where(edge_row == 0, before, after)
    slot = inv_ref[pl.ds(block, 1), :]
    taken = slot >= 0
    got = lane_take(change, jnp.broadcast_to(jnp.maximum(slot, 0), change.shape))
    value = jnp.where(taken, 0.5 * value + 0.5 * got[:rows], value)
    return value, jnp.where(taken, 0.5 * outer + 0.5 * got[rows:], outer)


def rim_kernel(
    planes, domains, count, dom_ref, mine_ref, recv_ref, table_ref, q_ref, inflow_ref, diag_ref, inv_ref,
    rim_ref, waves,
):
    nblocks = q_ref.shape[1] // LANES
    for side, block, pair in ((0, nblocks - 1, domains // 2 - 1), (1, 0, 0)):

        @pl.when(dom_ref[0] == side)
        def _(block=block, pair=pair):
            change = change_of((pair,), count, mine_ref, recv_ref, table_ref, waves)
            rim_ref[...] = pressure_block(planes, block, change, q_ref, inflow_ref, diag_ref, inv_ref)[0]


def pressure_kernel(
    planes, domains, count, mine_ref, recv_ref, table_ref, q_ref, inflow_ref, diag_ref, inv_ref,
    ext, change, waves,
):
    rows, cells = q_ref.shape
    nblocks = cells // LANES
    per_pair = 2 * nblocks // domains
    change[...] = change_of(range(domains // 2), count, mine_ref, recv_ref, table_ref, waves)

    def step(block, carry):
        column = pl.multiple_of((block // per_pair) * LANES, LANES)
        value, outer = pressure_block(
            planes, block, change[:, pl.ds(column, LANES)], q_ref, inflow_ref, diag_ref, inv_ref
        )
        here = pl.multiple_of((block + 1) * LANES, LANES)
        ext[pl.ds(SUB, rows), pl.ds(here, LANES)] = value
        ext[pl.ds(SUB - 1, 1), pl.ds(here, LANES)] = outer[0:1]
        ext[pl.ds(SUB + planes, 1), pl.ds(here, LANES)] = outer[1:2]
        return carry

    lax.fori_loop(0, nblocks, step, 0, unroll=4)


def corrected_kernel(ext_in, v_ref, halo_ref, sv_ref, fw_ref, nb_ref, p_hbm, out_ref, ext, sems):
    rows, cells = v_ref.shape
    nblocks = cells // LANES
    store = pltpu.make_async_copy(ext_in.at[pl.ds(SUB, rows), pl.ds(LANES, cells)], p_hbm, sems.at[0])
    store.start()
    ext[:, pl.ds(LANES, cells)] = ext_in[:, pl.ds(LANES, cells)]
    ext[pl.ds(SUB, rows), pl.ds(0, LANES)] = halo_ref[...]
    ext[pl.ds(SUB, rows), pl.ds(LANES + cells, LANES)] = halo_ref[...]

    def step(block, carry):
        start = pl.multiple_of(block * LANES, LANES)
        sv = sv_ref[:, pl.ds(start, LANES)]
        _, total = convection(ext, block, nblocks, rows, sv, fw_ref, nb_ref)
        out_ref[:, pl.ds(start, LANES)] = v_ref[:, pl.ds(start, LANES)] - total
        return carry

    lax.fori_loop(0, nblocks, step, 0, unroll=4)
    store.wait()


HBM = pl.BlockSpec(memory_space=pltpu.HBM)


def in_hbm(value):
    return pltpu.with_memory_space_constraint(value, pltpu.HBM)


PARAMS = pltpu.CompilerParams(vmem_limit_bytes=40 * 1024 * 1024)


def call(kernel, outs, args, scratch=(), specs=None, out_specs=None):
    return pl.pallas_call(
        kernel,
        out_shape=[jax.ShapeDtypeStruct(*out) for out in outs],
        in_specs=specs or whole(*args),
        out_specs=out_specs or whole(*outs),
        scratch_shapes=list(scratch),
        compiler_params=PARAMS,
    )(*(in_hbm(arg) if spec is HBM else arg for arg, spec in zip(args, specs or whole(*args))))


def inflow(ends, diag, planes):
    count, me = lax.axis_size("span"), lax.axis_index("span")
    lam, _ = decay(diag)
    step = lam
    for _ in range(int(math.log2(planes))):
        step = step * step
    squares = [step]
    while 2 ** len(squares) <= count:
        squares.append(squares[-1] * squares[-1])

    def power(exponent, bits):
        result = jnp.ones_like(step)
        for bit in range(bits):
            result = result * jnp.where((exponent >> bit) & 1 == 1, squares[bit], 1.0)
        return result

    left = jnp.zeros_like(step)
    right = jnp.zeros_like(step)
    ahead, back = ends[0], ends[1]
    bits = int(math.log2(count))
    for bit in range(bits):
        size = 1 << bit
        other = xor_permute(jnp.stack([ahead, back]), "span", size)
        is_right = (me >> bit) & 1 == 1
        place = me & (size - 1)
        reach = power(jnp.where(is_right, place, size - 1 - place), bit)
        left = jnp.where(is_right, left + reach * other[0], left)
        right = jnp.where(is_right, right, right + reach * other[1])
        ahead, back = (
            jnp.where(is_right, ahead + squares[bit] * other[0], other[0] + squares[bit] * ahead),
            jnp.where(is_right, other[1] + squares[bit] * back, back + squares[bit] * other[1]),
        )
    wrap = 1.0 / (1.0 - squares[bits])
    left = left + power(me, bits) * ahead * wrap
    right = right + power(count - 1 - me, bits) * back * wrap
    return left, right


def on_device(
    scalar, span_vel, flux_weight, neighbours, diagonal, interface, schur_one, schur_two, schur_three, schur_root
):
    planes, cells = scalar.shape
    count, me = lax.axis_size("span"), lax.axis_index("span")
    dom = lax.axis_index("dom")
    waves = schur_one.shape[0]
    rows, wave_rows = -(-planes // SUB) * SUB, -(-waves // SUB) * SUB
    nblocks = cells // LANES
    domains, slots = interface.shape
    pair_cells = domains // 2 * slots
    pad = lambda value: value if rows == planes else jnp.pad(value, ((0, rows - planes), (0, 0)))
    field, sv = pad(scalar), pad(span_vel)
    diag = diagonal.reshape(nblocks, LANES)
    offsets = xor_offsets(count)

    def boundary(value):
        edge = jnp.where(dom == 0, value[:, cells - LANES :], value[:, :LANES])
        return xor_permute(edge, "dom", 1)

    block_rows = 2 * rows + 3 * SUB
    vmem = pl.BlockSpec(memory_space=pltpu.VMEM)
    smem = pl.BlockSpec(memory_space=pltpu.SMEM)
    payload, local, edge, dif, field_in, sv_in, fw_in, nb_in, diag_in, iface_in = call(
        functools.partial(source_kernel, planes),
        [
            ((block_rows, 2 * LANES), F32),
            ((rows, cells), F32),
            ((6, nblocks, LANES), F32),
            ((domains, LANES), F32),
            ((rows, cells), F32),
            ((rows, cells), F32),
            (flux_weight.shape, F32),
            (neighbours.shape, jnp.int32),
            ((nblocks, LANES), F32),
            (interface.shape, jnp.int32),
        ],
        (boundary(field), field, sv, flux_weight, neighbours, diag, interface),
        [
            pltpu.VMEM((rows + 2 * SUB, cells + 2 * LANES), F32),
            pltpu.VMEM((SUB, cells), F32),
            pltpu.SemaphoreType.DMA((6,)),
        ],
        [vmem] + [HBM] * 6,
    )
    mine, received = gathered(payload, "span")

    slot_of, m1, flipped, m3, root = call(
        stage_kernel,
        [
            ((nblocks, LANES), jnp.int32),
            (schur_one.shape, F32),
            (schur_two.shape, F32),
            (schur_three.shape, F32),
            (schur_root.shape, F32),
        ],
        (iface_in, schur_one, schur_two, schur_three, schur_root),
        [pltpu.VMEM(schur_two.shape, F32), pltpu.SemaphoreType.DMA((4,))],
        [vmem] + [HBM] * 4,
    )
    own_wave = me * waves + jnp.arange(waves, dtype=jnp.int32)
    xored = me ^ jnp.array(offsets, jnp.int32)
    plane_of = xored[:, None] * planes + jnp.arange(rows, dtype=jnp.int32)[None, :]
    valid = jnp.arange(rows) < planes
    table = jnp.where(valid[None, None], fourier_entry(own_wave[:, None, None], plane_of[None]), 0.0)
    table = jnp.pad(table.reshape(waves, count * rows), ((0, wave_rows - waves), (0, 0)))
    edge_planes = (jnp.arange(count)[:, None] * planes + jnp.array([0, planes - 1])[None, :]).reshape(-1)
    edge_table = fourier_entry(own_wave[:, None], edge_planes[None, :].astype(jnp.int32))
    sigma = wave_shift(own_wave)
    s3, keep = call(
        functools.partial(up_kernel, offsets, rows),
        [((wave_rows, LANES), F32), ((waves, SUB, LANES), F32)],
        (me.reshape(1), mine, received, table, edge_table, sigma, dif, m1, flipped, m3),
        [
            pltpu.VMEM((count * rows, pair_cells), F32),
            pltpu.VMEM((count, 3 * SUB, 2 * LANES), F32),
            pltpu.VMEM((waves, SUB, LANES), F32),
            pltpu.VMEM((pair_cells // LANES, wave_rows, LANES), F32),
            pltpu.VMEM((LANES, LANES), F32),
        ],
        [smem, vmem, vmem, vmem, smem, smem] + [vmem] * 4,
    )
    other = xor_permute(s3, "dom", 1)
    (returned,) = call(
        down_kernel,
        [((pair_cells // LANES, wave_rows, LANES), F32)],
        (s3, other, keep, m1, flipped, m3, root),
        [pltpu.VMEM((LANES, LANES), F32)],
    )
    mine, received = gathered(returned.reshape(-1, LANES), "span")

    up_ring = [(i, (i + 1) % count) for i in range(count)]
    down_ring = [(j, i) for i, j in up_ring]
    q_first, q_last, v_first, v_last, sv_first, sv_last = (edge[i] for i in range(6))
    lam, kappa = decay(diag_in)
    v_before, v_after = lax.ppermute(v_last, "span", up_ring), lax.ppermute(v_first, "span", down_ring)
    at_first = kappa * 0.5 * sv_first * v_before
    at_last = -kappa * 0.5 * sv_last * v_after
    reach = jnp.ones_like(lam)
    for bit in range(int(math.log2(planes))):
        factor = lam
        for _ in range(bit):
            factor = factor * factor
        reach = reach * factor
    ends = jnp.stack([q_last + reach * at_first + at_last, q_first + at_first + reach * at_last])
    left, right = inflow(ends, diag_in, planes)
    flows = jnp.stack([left, right, at_first, at_last])

    wave_of = xored[:, None] * waves + jnp.arange(wave_rows, dtype=jnp.int32)[None, :]
    row_ids = jnp.arange(rows + SUB, dtype=jnp.int32)
    row_plane = jnp.where(row_ids < rows, row_ids, jnp.where(row_ids == rows, -1, planes))
    row_plane = (me * planes + row_plane + PLANES) % PLANES
    back_table = fourier_entry(wave_of[None], row_plane[:, None, None])
    back_table = jnp.where((jnp.arange(wave_rows) < waves)[None, None], back_table, 0.0)
    back_table = back_table.reshape(rows + SUB, count * wave_rows)
    wave_scratch = lambda pairs: pltpu.VMEM((count * wave_rows, pairs * LANES), F32)
    parts = (mine, received, back_table, local, flows, diag_in, slot_of)
    (rim,) = call(
        functools.partial(rim_kernel, planes, domains, count),
        [((rows, LANES), F32)],
        (dom.reshape(1),) + parts,
        [wave_scratch(1)],
        [smem] + [vmem] * 7,
    )
    halo = xor_permute(rim, "dom", 1)
    ext_shape = (rows + 2 * SUB, cells + 2 * LANES)
    (extended,) = call(
        functools.partial(pressure_kernel, planes, domains, count),
        [(ext_shape, F32)],
        parts,
        [pltpu.VMEM((rows + SUB, pair_cells), F32), wave_scratch(domains // 2)],
    )
    pressure, corrected = call(
        corrected_kernel,
        [((rows, cells), F32), ((rows, cells), F32)],
        (extended, field_in, halo, sv_in, fw_in, nb_in),
        [pltpu.VMEM(ext_shape, F32), pltpu.SemaphoreType.DMA((1,))],
        out_specs=[HBM, vmem],
    )
    return (pressure[:planes], corrected[:planes])


def solution(mesh):
    placed = (
        P(("case", "span"), "dom"),
        P(("case", "span"), "dom"),
        P(None, "dom"),
        P(None, "dom"),
        P("dom"),
        P("dom", None),
        P("span", "dom", None, None),
        P("span", "dom", None, None),
        P("span", "dom", None, None),
        P("span", None, None, None),
    )

    return jax.shard_map(
        on_device,
        mesh=mesh,
        in_specs=placed,
        out_specs=(P(("case", "span"), "dom"), P(("case", "span"), "dom")),
        check_vma=False,
    )
```

profile of v0, /device:TPU:0, one launch (start us, length us, event | category | flops | bytes accessed | tf_op | source)
XLA Modules:
  0.0 51.9 jit_solution(12587107050690685256)
XLA Ops:
  0.6 0.7 %slice_select_fusion = f32[16,128]{1,0:T(8,128)S(1)} fusion(f32[16,4096]{1,0:T(8,128)} %v_hbm.1, pred[]{:T(512)S(6)} %eq.95), kind=kLoop, calls=%fused_computation.88 | loop fusion | flops 2048 | bytes 24577 | tf_op jit(solution)/shard_map/jit(_where)/select_n | solution.py:474
  1.4 0.5 collective-permute-start
  1.9 0.7 %xor_multiply_fusion = s32[8]{0:T(128)S(1)} fusion(s32[8]{0:T(128)} %constant.104.clone, s32[]{:T(128)} %axis_index.27), kind=kLoop, calls=%fused_computation.106 | loop fusion | flops 16 | bytes 68 | tf_op jit(solution)/shard_map/mul | solution.py:519
  3.1 0.1 multiply_select_fusion.7.table_ref
  3.3 0.1 multiply_select_fusion.6.table_ref
  3.5 3.1 %shard_map.131 = (f32[56,256]{1,0:T(8,128)S(1)}, f32[16,4096]{1,0:T(8,128)S(1)}, f32[6,32,128]{2,1,0:T(8,128)S(1)}, f32[8,128]{1,0:T(8,128)S(1)}, f32[16,4096]{1...) custom-call(f32[16,128]{1,0:T(8,128)S(1)} %collective-permute-done.h, ...), custom_call_target="tpu_custom_call" | custom-call | tf_op jit(solution)/shard_map/pallas_call | solution.py:409
  6.6 2.6 %collective-permute-start.10 = (f32[32,128]{1,0:T(8,128)S(1)}, f32[32,128]{1,0:T(8,128)S(1)}, u32[]{:S(2)}, u32[]{:S(2)}) collective-permute-start(f32[32,128]{1,0:T(8,128)S(1)} %get-tuple-element.44), channel_id=1, source_target_pairs={{0,2},{2,4},{4,6},{6,8},{8,10},{10,12},{12,14},{14,0},{1,3},{3,5},... | collective-permute-start | bytes 49160 | tf_op jit(solution)/shard_map/ppermute | solution.py:552
  9.2 3.1 %collective-permute-start.11 = (f32[32,128]{1,0:T(8,128)S(1)}, f32[32,128]{1,0:T(8,128)S(1)}, u32[]{:S(2)}, u32[]{:S(2)}) collective-permute-start(f32[32,128]{1,0:T(8,128)S(1)} %get-tuple-element.43), channel_id=1, source_target_pairs={{2,0},{4,2},{6,4},{8,6},{10,8},{12,10},{14,12},{0,14},{3,1},{5,3},... | collective-permute-start | bytes 49160 | tf_op jit(solution)/shard_map/ppermute | solution.py:552
  12.3 2.5 %collective-permute-start.2 = (f32[56,256]{1,0:T(8,128)S(1)}, f32[56,256]{1,0:T(8,128)S(1)}, u32[]{:S(2)}, u32[]{:S(2)}) collective-permute-start(f32[56,256]{1,0:T(8,128)S(1)} %get-tuple-element.19), channel_id=1, source_target_pairs={{0,8},{2,10},{4,12},{6,14},{8,0},{10,2},{12,4},{14,6},{1,9},{3,11}... | collective-permute-start | bytes 172040 | tf_op jit(solution)/shard_map/ppermute | solution.py:36
  14.8 1.9 %collective-permute-start.3 = (f32[56,256]{1,0:T(8,128)S(1)}, f32[56,256]{1,0:T(8,128)S(1)}, u32[]{:S(2)}, u32[]{:S(2)}) collective-permute-start(f32[56,256]{1,0:T(8,128)S(1)} %get-tuple-element.19), channel_id=1, source_target_pairs={{0,12},{2,14},{4,8},{6,10},{8,4},{10,6},{12,0},{14,2},{1,13},{3,15... | collective-permute-start | bytes 172040 | tf_op jit(solution)/shard_map/ppermute | solution.py:36
  16.9 0.5 collective-permute-done.1
  17.3 2.4 %collective-permute-done.2 = f32[56,256]{1,0:T(8,128)S(1)} collective-permute-done((f32[56,256]{1,0:T(8,128)S(1)}, f32[56,256]{1,0:T(8,128)S(1)}, u32[]{:S(2)}, u32[]{:S(2)}) %collective-permute-start.2) | collective-permute-done | bytes 57376 | tf_op jit(solution)/shard_map/ppermute | solution.py:36
  19.8 1.1 %collective-permute-done.3 = f32[56,256]{1,0:T(8,128)S(1)} collective-permute-done((f32[56,256]{1,0:T(8,128)S(1)}, f32[56,256]{1,0:T(8,128)S(1)}, u32[]{:S(2)}, u32[]{:S(2)}) %collective-permute-start.3) | collective-permute-done | bytes 57376 | tf_op jit(solution)/shard_map/ppermute | solution.py:36
  20.9 0.5 %collective-permute-start.4 = (f32[224,256]{1,0:T(8,128)S(1)}, f32[224,256]{1,0:T(8,128)S(1)}, u32[]{:S(2)}, u32[]{:S(2)}) collective-permute-start(f32[224,256]{1,0:T(8,128)S(1)} %constant_dynamic-update-slice_fusion.mine_ref), channel_id=1, source_target_pairs={{0,2},{2,0},{4,6},{6,4},{8,10},{10,8},{12,14},{14,12},{1,3},{3,1},... | collective-permute-start | bytes 688136 | tf_op jit(solution)/shard_map/ppermute | solution.py:36
  21.4 0.3 collective-permute-start.13
  21.8 3.4 %shard_map.132 = (s32[32,128]{1,0:T(8,128)S(1)}, f32[16,4,128,128]{3,2,1,0:T(8,128)S(1)}, f32[16,2,128,128]{3,2,1,0:T(8,128)S(1)}, f32[16,1,128,128]{3,2,1,0:T(8,128)S(1)}, f32[16,1,128,128]{3,2,1,0:T(8,128)S(1)}) custom-call(s32[8,128]{1,0:T(8,128)S(1)} %get-tuple-element.21.iface_ref, f32[16,4,128,128]{3,2,1,0:T(8,128)} %m1_hbm.1, ...), custom_call_target="tpu_custom_call" | custom-call | tf_op jit(solution)/shard_map/pallas_call | solution.py:409
  25.2 1.7 %collective-permute-done.4.recv_ref = f32[224,256]{1,0:T(8,128)S(1)} collective-permute-done((f32[224,256]{1,0:T(8,128)S(1)}, f32[224,256]{1,0:T(8,128)S(1)}, u32[]{:S(2)}, u32[]{:S(2)}) %collective-permute-start.4) | collective-permute-done | bytes 229408 | tf_op jit(solution)/shard_map/ppermute | solution.py:36
  26.9 3.8 %shard_map.133 = (f32[16,128]{1,0:T(8,128)S(1)}, f32[16,8,128]{2,1,0:T(8,128)S(1)}) custom-call(s32[1]{0:T(128)} %bitcast.me_ref, f32[224,256]{1,0:T(8,128)S(1)} %constant_dynamic-update-slice_fusion.mine_ref, f32[224,256]{1,0:T(8,128)S(1)} %collective-permute-done.4.recv_ref, f32[16,128]{1,0:T(8,128)S(1)} %multiply_select_fusion.7.table_ref, ...), custom_call_target="tpu_custom_call" | custom-call | tf_op jit(solution)/shard_map/pallas_call | solution.py:409
  30.8 1.1 %collective-permute-done.5.other_ref = f32[16,128]{1,0:T(8,128)S(1)} collective-permute-done((f32[16,128]{1,0:T(8,128)S(1)}, f32[16,128]{1,0:T(8,128)S(1)}, u32[]{:S(2)}, u32[]{:S(2)}) %collective-permute-start.5) | collective-permute-done | bytes 8224 | tf_op jit(solution)/shard_map/ppermute | solution.py:36
  31.9 2.9 %shard_map.134 = f32[4,16,128]{2,1,0:T(8,128)S(1)} custom-call(f32[16,128]{1,0:T(8,128)S(1)} %get-tuple-element.25.s3_ref, f32[16,128]{1,0:T(8,128)S(1)} %collective-permute-done.5.other_ref, f32[16,8,128]{2,1,0:T(8,128)S(1)} %get-tuple-element.26.keep_ref, f32[16,4,128,128]{3,2,1,0:T(8,128)S(1)} %get-tuple-element.22.m1, ...), custom_call_target="tpu_custom_call" | custom-call | tf_op jit(solution)/shard_map/pallas_call | solution.py:409
  34.8 0.8 %collective-permute-start.6 = (f32[64,128]{1,0:T(8,128)S(1)}, f32[64,128]{1,0:T(8,128)S(1)}, u32[]{:S(2)}, u32[]{:S(2)}) collective-permute-start(f32[64,128]{1,0:T(8,128)S(1)} %bitcast.82), channel_id=1, source_target_pairs={{0,4},{2,6},{4,0},{6,2},{8,12},{10,14},{12,8},{14,10},{1,5},{3,7},... | collective-permute-start | bytes 98312 | tf_op jit(solution)/shard_map/ppermute | solution.py:36
  35.6 1.8 %collective-permute-start.7 = (f32[64,128]{1,0:T(8,128)S(1)}, f32[64,128]{1,0:T(8,128)S(1)}, u32[]{:S(2)}, u32[]{:S(2)}) collective-permute-start(f32[64,128]{1,0:T(8,128)S(1)} %bitcast.83), channel_id=1, source_target_pairs={{0,8},{2,10},{4,12},{6,14},{8,0},{10,2},{12,4},{14,6},{1,9},{3,11}... | collective-permute-start | bytes 98312 | tf_op jit(solution)/shard_map/ppermute | solution.py:36
  37.3 1.9 %collective-permute-start.8 = (f32[64,128]{1,0:T(8,128)S(1)}, f32[64,128]{1,0:T(8,128)S(1)}, u32[]{:S(2)}, u32[]{:S(2)}) collective-permute-start(f32[64,128]{1,0:T(8,128)S(1)} %bitcast.84), channel_id=1, source_target_pairs={{0,12},{2,14},{4,8},{6,10},{8,4},{10,6},{12,0},{14,2},{1,13},{3,15... | collective-permute-start | bytes 98312 | tf_op jit(solution)/shard_map/ppermute | solution.py:36
  39.2 0.6 %collective-permute-start.14 = (f32[2,32,128]{2,1,0:T(8,128)S(1)}, f32[2,32,128]{2,1,0:T(8,128)S(1)}, u32[]{:S(2)}, u32[]{:S(2)}) collective-permute-start(f32[2,32,128]{2,1,0:T(8,128)S(1)} %pad_maximum_fusion.4), channel_id=1, source_target_pairs={{0,8},{2,10},{4,12},{6,14},{8,0},{10,2},{12,4},{14,6},{1,9},{3,11}... | collective-permute-start | bytes 98312 | tf_op jit(solution)/shard_map/ppermute | solution.py:36
  39.8 0.9 %collective-permute-done.7 = f32[64,128]{1,0:T(8,128)S(1)} collective-permute-done((f32[64,128]{1,0:T(8,128)S(1)}, f32[64,128]{1,0:T(8,128)S(1)}, u32[]{:S(2)}, u32[]{:S(2)}) %collective-permute-start.7) | collective-permute-done | bytes 32800 | tf_op jit(solution)/shard_map/ppermute | solution.py:36
  40.7 2.4 %collective-permute-done.8 = f32[64,128]{1,0:T(8,128)S(1)} collective-permute-done((f32[64,128]{1,0:T(8,128)S(1)}, f32[64,128]{1,0:T(8,128)S(1)}, u32[]{:S(2)}, u32[]{:S(2)}) %collective-permute-start.8) | collective-permute-done | bytes 32800 | tf_op jit(solution)/shard_map/ppermute | solution.py:36
  43.1 0.5 collective-permute-start.9
  43.6 0.4 collective-permute-done.14
  44.1 4.0 %collective-permute-done.9.recv_ref = f32[256,128]{1,0:T(8,128)S(1)} collective-permute-done((f32[256,128]{1,0:T(8,128)S(1)}, f32[256,128]{1,0:T(8,128)S(1)}, u32[]{:S(2)}, u32[]{:S(2)}) %collective-permute-start.9) | collective-permute-done | bytes 131104 | tf_op jit(solution)/shard_map/ppermute | solution.py:36
  48.1 0.2 shard_map.136
  48.4 1.1 %shard_map.135.ext_in = f32[32,4352]{1,0:T(8,128)S(1)} custom-call(f32[256,128]{1,0:T(8,128)S(1)} %pad_maximum_fusion.mine_ref, f32[256,128]{1,0:T(8,128)S(1)} %collective-permute-done.9.recv_ref, f32[24,128]{1,0:T(8,128)S(1)} %multiply_select_fusion.6.table_ref, f32[16,4096]{1,0:T(8,128)S(1)} %get-tuple-element.28.q_ref, ...), custom_call_target="tpu_custom_call" | custom-call | tf_op jit(solution)/shard_map/pallas_call | solution.py:409
  49.6 2.3 %shard_map.137 = (f32[16,4096]{1,0:T(8,128)}, f32[16,4096]{1,0:T(8,128)}) custom-call(f32[32,4352]{1,0:T(8,128)S(1)} %shard_map.135.ext_in, f32[16,4096]{1,0:T(8,128)S(1)} %get-tuple-element.32.v_ref, f32[16,128]{1,0:T(8,128)S(1)} %collective-permute-done.15.halo_ref, f32[16,4096]{1,0:T(8,128)S(1)} %get-tuple-element.33.sv_ref, ...), custom_call_target="tpu_custom_call" | custom-call | tf_op jit(solution)/shard_map/pallas_call | solution.py:409
  (46 shorter events, 1.2 us)
Async XLA Ops:
  1.4 2.2 %collective-permute-start = (f32[16,128]{1,0:T(8,128)S(1)}, f32[16,128]{1,0:T(8,128)S(1)}, u32[]{:S(2)}, u32[]{:S(2)}) collective-permute-start(f32[16,128]{1,0:T(8,128)S(1)} %slice_select_fusion), channel_id=1, source_target_pairs={{0,1},{1,0},{2,3},{3,2},{4,5},{5,4},{6,7},{7,6},{8,9},{9,8},{10,11... | collective-permute-start | bytes 24584 | tf_op jit(solution)/shard_map/ppermute | solution.py:36
  6.6 10.1 %collective-permute-start.10 = (f32[32,128]{1,0:T(8,128)S(1)}, f32[32,128]{1,0:T(8,128)S(1)}, u32[]{:S(2)}, u32[]{:S(2)}) collective-permute-start(f32[32,128]{1,0:T(8,128)S(1)} %get-tuple-element.44), channel_id=1, source_target_pairs={{0,2},{2,4},{4,6},{6,8},{8,10},{10,12},{12,14},{14,0},{1,3},{3,5},... | collective-permute-start | bytes 49160 | tf_op jit(solution)/shard_map/ppermute | solution.py:552
  9.2 7.5 %collective-permute-start.11 = (f32[32,128]{1,0:T(8,128)S(1)}, f32[32,128]{1,0:T(8,128)S(1)}, u32[]{:S(2)}, u32[]{:S(2)}) collective-permute-start(f32[32,128]{1,0:T(8,128)S(1)} %get-tuple-element.43), channel_id=1, source_target_pairs={{2,0},{4,2},{6,4},{8,6},{10,8},{12,10},{14,12},{0,14},{3,1},{5,3},... | collective-permute-start | bytes 49160 | tf_op jit(solution)/shard_map/ppermute | solution.py:552
  12.3 5.0 %collective-permute-start.1 = (f32[56,256]{1,0:T(8,128)S(1)}, f32[56,256]{1,0:T(8,128)S(1)}, u32[]{:S(2)}, u32[]{:S(2)}) collective-permute-start(f32[56,256]{1,0:T(8,128)S(1)} %get-tuple-element.19), channel_id=1, source_target_pairs={{0,4},{2,6},{4,0},{6,2},{8,12},{10,14},{12,8},{14,10},{1,5},{3,7},... | collective-permute-start | bytes 172040 | tf_op jit(solution)/shard_map/ppermute | solution.py:36
  12.3 7.5 %collective-permute-start.2 = (f32[56,256]{1,0:T(8,128)S(1)}, f32[56,256]{1,0:T(8,128)S(1)}, u32[]{:S(2)}, u32[]{:S(2)}) collective-permute-start(f32[56,256]{1,0:T(8,128)S(1)} %get-tuple-element.19), channel_id=1, source_target_pairs={{0,8},{2,10},{4,12},{6,14},{8,0},{10,2},{12,4},{14,6},{1,9},{3,11}... | collective-permute-start | bytes 172040 | tf_op jit(solution)/shard_map/ppermute | solution.py:36
  14.8 6.1 %collective-permute-start.3 = (f32[56,256]{1,0:T(8,128)S(1)}, f32[56,256]{1,0:T(8,128)S(1)}, u32[]{:S(2)}, u32[]{:S(2)}) collective-permute-start(f32[56,256]{1,0:T(8,128)S(1)} %get-tuple-element.19), channel_id=1, source_target_pairs={{0,12},{2,14},{4,8},{6,10},{8,4},{10,6},{12,0},{14,2},{1,13},{3,15... | collective-permute-start | bytes 172040 | tf_op jit(solution)/shard_map/ppermute | solution.py:36
  16.8 4.6 %collective-permute-start.12 = (f32[2,32,128]{2,1,0:T(8,128)S(1)}, f32[2,32,128]{2,1,0:T(8,128)S(1)}, u32[]{:S(2)}, u32[]{:S(2)}) collective-permute-start(f32[2,32,128]{2,1,0:T(8,128)S(1)} %pad_maximum_fusion.2), channel_id=1, source_target_pairs={{0,2},{2,0},{4,6},{6,4},{8,10},{10,8},{12,14},{14,12},{1,3},{3,1},... | collective-permute-start | bytes 98312 | tf_op jit(solution)/shard_map/ppermute | solution.py:36
  20.9 6.0 %collective-permute-start.4 = (f32[224,256]{1,0:T(8,128)S(1)}, f32[224,256]{1,0:T(8,128)S(1)}, u32[]{:S(2)}, u32[]{:S(2)}) collective-permute-start(f32[224,256]{1,0:T(8,128)S(1)} %constant_dynamic-update-slice_fusion.mine_ref), channel_id=1, source_target_pairs={{0,2},{2,0},{4,6},{6,4},{8,10},{10,8},{12,14},{14,12},{1,3},{3,1},... | collective-permute-start | bytes 688136 | tf_op jit(solution)/shard_map/ppermute | solution.py:36
  21.4 9.3 %collective-permute-start.13 = (f32[2,32,128]{2,1,0:T(8,128)S(1)}, f32[2,32,128]{2,1,0:T(8,128)S(1)}, u32[]{:S(2)}, u32[]{:S(2)}) collective-permute-start(f32[2,32,128]{2,1,0:T(8,128)S(1)} %pad_maximum_fusion.3), channel_id=1, source_target_pairs={{0,4},{2,6},{4,0},{6,2},{8,12},{10,14},{12,8},{14,10},{1,5},{3,7},... | collective-permute-start | bytes 98312 | tf_op jit(solution)/shard_map/ppermute | solution.py:36
  30.7 1.2 %collective-permute-start.5 = (f32[16,128]{1,0:T(8,128)S(1)}, f32[16,128]{1,0:T(8,128)S(1)}, u32[]{:S(2)}, u32[]{:S(2)}) collective-permute-start(f32[16,128]{1,0:T(8,128)S(1)} %get-tuple-element.25.s3_ref), channel_id=1, source_target_pairs={{0,1},{1,0},{2,3},{3,2},{4,5},{5,4},{6,7},{7,6},{8,9},{9,8},{10,11... | collective-permute-start | bytes 24584 | tf_op jit(solution)/shard_map/ppermute | solution.py:36
  34.8 5.0 %collective-permute-start.6 = (f32[64,128]{1,0:T(8,128)S(1)}, f32[64,128]{1,0:T(8,128)S(1)}, u32[]{:S(2)}, u32[]{:S(2)}) collective-permute-start(f32[64,128]{1,0:T(8,128)S(1)} %bitcast.82), channel_id=1, source_target_pairs={{0,4},{2,6},{4,0},{6,2},{8,12},{10,14},{12,8},{14,10},{1,5},{3,7},... | collective-permute-start | bytes 98312 | tf_op jit(solution)/shard_map/ppermute | solution.py:36
  35.6 5.2 %collective-permute-start.7 = (f32[64,128]{1,0:T(8,128)S(1)}, f32[64,128]{1,0:T(8,128)S(1)}, u32[]{:S(2)}, u32[]{:S(2)}) collective-permute-start(f32[64,128]{1,0:T(8,128)S(1)} %bitcast.83), channel_id=1, source_target_pairs={{0,8},{2,10},{4,12},{6,14},{8,0},{10,2},{12,4},{14,6},{1,9},{3,11}... | collective-permute-start | bytes 98312 | tf_op jit(solution)/shard_map/ppermute | solution.py:36
  37.3 5.8 %collective-permute-start.8 = (f32[64,128]{1,0:T(8,128)S(1)}, f32[64,128]{1,0:T(8,128)S(1)}, u32[]{:S(2)}, u32[]{:S(2)}) collective-permute-start(f32[64,128]{1,0:T(8,128)S(1)} %bitcast.84), channel_id=1, source_target_pairs={{0,12},{2,14},{4,8},{6,10},{8,4},{10,6},{12,0},{14,2},{1,13},{3,15... | collective-permute-start | bytes 98312 | tf_op jit(solution)/shard_map/ppermute | solution.py:36
  39.2 4.8 %collective-permute-start.14 = (f32[2,32,128]{2,1,0:T(8,128)S(1)}, f32[2,32,128]{2,1,0:T(8,128)S(1)}, u32[]{:S(2)}, u32[]{:S(2)}) collective-permute-start(f32[2,32,128]{2,1,0:T(8,128)S(1)} %pad_maximum_fusion.4), channel_id=1, source_target_pairs={{0,8},{2,10},{4,12},{6,14},{8,0},{10,2},{12,4},{14,6},{1,9},{3,11}... | collective-permute-start | bytes 98312 | tf_op jit(solution)/shard_map/ppermute | solution.py:36
  43.1 5.0 %collective-permute-start.9 = (f32[256,128]{1,0:T(8,128)S(1)}, f32[256,128]{1,0:T(8,128)S(1)}, u32[]{:S(2)}, u32[]{:S(2)}) collective-permute-start(f32[256,128]{1,0:T(8,128)S(1)} %pad_maximum_fusion.mine_ref), channel_id=1, source_target_pairs={{0,2},{2,0},{4,6},{6,4},{8,10},{10,8},{12,14},{14,12},{1,3},{3,1},... | collective-permute-start | bytes 393224 | tf_op jit(solution)/shard_map/ppermute | solution.py:36
  48.4 1.2 %collective-permute-start.15 = (f32[16,128]{1,0:T(8,128)S(1)}, f32[16,128]{1,0:T(8,128)S(1)}, u32[]{:S(2)}, u32[]{:S(2)}) collective-permute-start(f32[16,128]{1,0:T(8,128)S(1)} %shard_map.136), channel_id=1, source_target_pairs={{0,1},{1,0},{2,3},{3,2},{4,5},{5,4},{6,7},{7,6},{8,9},{9,8},{10,11... | collective-permute-start | bytes 24584 | tf_op jit(solution)/shard_map/ppermute | solution.py:36
where the time goes:
time: 52 us; the launch traced here: 51.9 us
  starting transfers between devices  17 us (33%)
  Pallas kernels  16.7 us (32%)
  waiting for transfers between devices  14.6 us (28%)
  other arithmetic  2.16 us (4%)
  between operations  0.89 us (2%)
    pallas_call x7, Pallas kernels, call(): pl.pallas_call(kernel, out_shape=[jax.ShapeDtypeStruct(*out) for out in o...  16.7 us
    ppermute x14, waiting for transfers between devices, xor_permute(): lax.ppermute(value, axis, [(i, i ^ mask) for i in range(lax.axis_size(axi...  14.6 us
    ppermute x14, starting transfers between devices, xor_permute(): lax.ppermute(value, axis, [(i, i ^ mask) for i in range(lax.axis_size(axi...  11.4 us
    ppermute x1, starting transfers between devices, on_device(): lax.ppermute(v_first, 'span', down_ring)  3.1 us
    ppermute x1, starting transfers between devices, on_device(): lax.ppermute(v_last, 'span', up_ring)  2.57 us
  transfers between devices with their start and end apart: 16, of which 10 were waited for; matrix products, arithmetic and copies ran while one was open for 4% of the time, Pallas kernels for 16%

commit v1 on v0

--- a/solution.py
+++ b/solution.py
@@ -13,7 +13,9 @@
 LANES = 128
 SUB = 8
 HALF = LANES // 2
+GROUP = 8
 F32 = jnp.float32
+BF16 = jnp.bfloat16
 EXACT = lax.Precision.HIGHEST
 
 
@@ -71,12 +73,15 @@
     return result
 
 
-def convection(ext, block, nblocks, rows, sv, fw_ref, nb_ref):
-    start = pl.multiple_of(block * LANES, LANES)
-    here = pl.multiple_of(start + LANES, LANES)
+def column(block):
+    return block * LANES if isinstance(block, int) else pl.multiple_of(block * LANES, LANES)
+
+
+def convection(ext, at, block, nblocks, rows, sv, fw_ref, nb_ref):
+    start, here = column(block), column(at)
     field = ext[pl.ds(SUB, rows), pl.ds(here, LANES)]
-    before = ext[pl.ds(SUB, rows), pl.ds(start, LANES)]
-    after = ext[pl.ds(SUB, rows), pl.ds(pl.multiple_of(here + LANES, LANES), LANES)]
+    before = ext[pl.ds(SUB, rows), pl.ds(column(at - 1), LANES)]
+    after = ext[pl.ds(SUB, rows), pl.ds(column(at + 1), LANES)]
     lane = lax.broadcasted_iota(jnp.int32, (rows, LANES), 1)
     around = jnp.where(lane < HALF, after, before)
     ahead = ext[pl.ds(SUB + 1, rows), pl.ds(here, LANES)]
@@ -91,58 +96,81 @@
     return field, total
 
 
-def fill(ext, field_ref, halo_ref, rows, cells):
-    ext[pl.ds(SUB, rows), pl.ds(LANES, cells)] = field_ref[...]
-    ext[pl.ds(SUB, rows), pl.ds(0, LANES)] = halo_ref[...]
-    ext[pl.ds(SUB, rows), pl.ds(LANES + cells, LANES)] = halo_ref[...]
+def source_block(planes, ext, at, block, sv_ref, fw_ref, nb_ref, diag_ref, q_ref, edge_ref, strip):
+    rows = q_ref.shape[0]
+    nblocks = diag_ref.shape[0]
+    row = lax.broadcasted_iota(jnp.int32, (rows, LANES), 0)
+    start = column(block)
+    sv = sv_ref[:, pl.ds(start, LANES)]
+    field, total = convection(ext, at, block, nblocks, rows, sv, fw_ref, nb_ref)
+    source = field - total
+    diag = diag_ref[pl.ds(block, 1), :]
+    lam, kappa = decay(diag)
+    forward, backward, factor, shift = source, source, lam, 1
+    while shift < planes:
+        down = jnp.where(row >= shift, pltpu.roll(forward, shift, 0), 0.0)
+        up = jnp.where(row < rows - shift, pltpu.roll(backward, rows - shift, 0), 0.0)
+        forward = forward + factor * down
+        backward = backward + factor * up
+        factor, shift = factor * factor, shift * 2
+    local = kappa * (forward + (backward - source))
+    q_ref[:, pl.ds(start, LANES)] = local
+    last = planes - 1
+    edges = (
+        local[0:1], local[last:planes], sv[0:1], sv[last:planes], field[0:1], field[last:planes], diag,
+    )
+    for place, value in enumerate(edges):
+        strip[pl.ds(place, 1), pl.ds(start, LANES)] = value
+        if place < edge_ref.shape[0]:
+            edge_ref[place, pl.ds(block, 1), :] = value
 
 
 def source_kernel(
-    planes, halo_ref, v_hbm, sv_hbm, fw_hbm, nb_hbm, diag_hbm, iface_hbm,
-    pay_ref, q_ref, edge_ref, dif_ref, v_ref, sv_ref, fw_ref, nb_ref, diag_ref, iface_ref, ext, strip, sems,
+    planes, v_hbm, sv_hbm, fw_hbm, nb_hbm, diag_hbm, iface_hbm,
+    q_ref, edge_ref, strip, ext, v_ref, sv_ref, fw_ref, nb_ref, diag_ref, iface_ref, sems,
 ):
     rows, cells = v_ref.shape
+    nblocks = cells // LANES
     moved = (
         (v_hbm, v_ref), (sv_hbm, sv_ref), (fw_hbm, fw_ref), (nb_hbm, nb_ref), (diag_hbm, diag_ref), (iface_hbm, iface_ref),
     )
     moves = [pltpu.make_async_copy(src, dst, sems.at[i]) for i, (src, dst) in enumerate(moved)]
     for move in moves:
         move.start()
+    ext[pl.ds(0, SUB), :] = jnp.zeros((SUB, cells + 2 * LANES), F32)
+    ext[pl.ds(SUB + rows, SUB), :] = jnp.zeros((SUB, cells + 2 * LANES), F32)
+    for side in (0, LANES + cells):
+        ext[pl.ds(SUB, rows), pl.ds(side, LANES)] = jnp.zeros((rows, LANES), F32)
     for move in moves:
         move.wait()
+    ext[pl.ds(SUB, rows), pl.ds(LANES, cells)] = v_ref[...]
+
+    def step(block, carry):
+        source_block(
+            planes, ext, block + 1, block, sv_ref, fw_ref, nb_ref, diag_ref, q_ref, edge_ref, strip
+        )
+        return carry
+
+    lax.fori_loop(0, nblocks, step, 0, unroll=4)
+
+
+def seam_kernel(
+    planes, dom_ref, halo_ref, q_in, edge_in, strip_in, ext, sv_ref, fw_ref, nb_ref, diag_ref, iface_ref,
+    q_ref, edge_ref, strip, pay_ref, dif_ref, window,
+):
+    rows, cells = q_ref.shape
     nblocks = cells // LANES
-    fill(ext, v_ref, halo_ref, rows, cells)
-    ext[pl.ds(0, SUB), :] = jnp.zeros((SUB, cells + 2 * LANES), F32)
-    ext[pl.ds(SUB + rows, SUB), :] = jnp.zeros((SUB, cells + 2 * LANES), F32)
-    row = lax.broadcasted_iota(jnp.int32, (rows, LANES), 0)
-
-    def step(block, carry):
-        start = pl.multiple_of(block * LANES, LANES)
-        sv = sv_ref[:, pl.ds(start, LANES)]
-        field, total = convection(ext, block, nblocks, rows, sv, fw_ref, nb_ref)
-        source = field - total
-        diag = diag_ref[pl.ds(block, 1), :]
-        lam, kappa = decay(diag)
-        forward, backward, factor, shift = source, source, lam, 1
-        while shift < planes:
-            down = jnp.where(row >= shift, pltpu.roll(forward, shift, 0), 0.0)
-            up = jnp.where(row < rows - shift, pltpu.roll(backward, rows - shift, 0), 0.0)
-            forward = forward + factor * down
-            backward = backward + factor * up
-            factor, shift = factor * factor, shift * 2
-        local = kappa * (forward + (backward - source))
-        q_ref[:, pl.ds(start, LANES)] = local
-        last = planes - 1
-        edges = (
-            local[0:1], local[last:planes], field[0:1], field[last:planes], sv[0:1], sv[last:planes], diag,
-        )
-        for place, value in enumerate(edges):
-            strip[pl.ds(place, 1), pl.ds(start, LANES)] = value
-            if place < 6:
-                edge_ref[place, pl.ds(block, 1), :] = value
-        return carry
-
-    lax.fori_loop(0, nblocks, step, 0, unroll=4)
+    for side, block in ((0, nblocks - 1), (1, 0)):
+
+        @pl.when(dom_ref[0] == side)
+        def _(side=side, block=block):
+            near = side * LANES
+            window[:, pl.ds(near, 2 * LANES)] = ext[:, pl.ds(column(block + side), 2 * LANES)]
+            window[pl.ds(SUB, rows), pl.ds(2 * LANES * (1 - side), LANES)] = halo_ref[...]
+            source_block(
+                planes, window, 1, block, sv_ref, fw_ref, nb_ref, diag_ref, q_ref, edge_ref, strip
+            )
+
     domains = iface_ref.shape[0]
     width = cells // domains
     for pair in range(domains // 2):
@@ -164,8 +192,8 @@
                 at = 2 * rows + SUB * (place // 2) + domain
                 pay_ref[pl.ds(at, 1), pl.ds((place % 2) * LANES, LANES)] = outer[place : place + 1]
             dif_ref[pl.ds(domain, 1), :] = outer[6:7]
-        half, column = divmod(pair, domains // 4)
-        pay_ref[pl.ds(half * rows, rows), pl.ds(column * LANES, LANES)] = total
+        half, side = divmod(pair, domains // 4)
+        pay_ref[pl.ds(half * rows, rows), pl.ds(side * LANES, LANES)] = total
 
 
 def slots_of(iface_ref, inv_ref):
@@ -183,37 +211,62 @@
             inv_ref[pl.ds(domain * per + part, 1), :] = found.astype(jnp.int32)
 
 
+def split(value):
+    high = value.astype(BF16)
+    return high, (value - high.astype(F32)).astype(BF16)
+
+
 def stage_kernel(
-    iface_ref, m1_hbm, m2_hbm, m3_hbm, root_hbm, inv_ref, m1, flipped, m3, root, m2, sems
+    iface_ref, m1_hbm, m2_hbm, m3_hbm, root_hbm, inv_ref, s1, s2, s3, s0, m1, m2, m3, root, sems
 ):
-    moved = ((m2_hbm, m2), (m1_hbm, m1), (m3_hbm, m3), (root_hbm, root))
-    moves = [pltpu.make_async_copy(src, dst, sems.at[i]) for i, (src, dst) in enumerate(moved)]
-    for move in moves:
-        move.start()
+    waves = m1.shape[0]
+    moved = ((m3_hbm, m3, s3), (root_hbm, root, s0), (m2_hbm, m2, s2), (m1_hbm, m1, s1))
+    chunks = [(source, 0, waves) for source in range(3)]
+    size = waves // math.gcd(waves, 4)
+    chunks += [(3, first, size) for first in range(0, waves, size)]
+    moves = []
+    for place, (source, first, size) in enumerate(chunks):
+        src, dst, _ = moved[source]
+        moves.append(
+            pltpu.make_async_copy(src.at[pl.ds(first, size)], dst.at[pl.ds(first, size)], sems.at[place])
+        )
+        moves[-1].start()
     slots_of(iface_ref, inv_ref)
-    moves[0].wait()
-
-    def flip(wave, carry):
-        for node in range(m2.shape[1]):
-            flipped[wave, node] = jnp.transpose(m2[wave, node])
-        return carry
-
-    lax.fori_loop(0, m2.shape[0], flip, 0, unroll=2)
-    for move in moves[1:]:
+    for move, (source, first, size) in zip(moves, chunks):
+        _, whole_ref, parts_ref = moved[source]
         move.wait()
 
-
-def over_lanes(matrix, row):
-    return jnp.sum(matrix * row, axis=1, keepdims=True)
-
-
-def over_rows(matrix, column):
-    return jnp.sum(matrix * column, axis=0, keepdims=True)
+        def part(wave, carry, whole_ref=whole_ref, parts_ref=parts_ref):
+            for node in range(whole_ref.shape[1]):
+                parts_ref[wave, node, 0], parts_ref[wave, node, 1] = split(whole_ref[wave, node])
+            return carry
+
+        lax.fori_loop(first, first + size, part, 0, unroll=max(1, 4 // whole_ref.shape[1]))
+
+
+def matvecs(vectors, matrices, flipped):
+    row = lax.broadcasted_iota(jnp.int32, (SUB, LANES), 0)
+    results = []
+    for one in range(0, len(vectors), 2):
+        both = first = jnp.zeros((SUB, LANES), F32)
+        for place, vector in enumerate(vectors[one : one + 2]):
+            high = vector.astype(BF16).astype(F32)
+            first = jnp.where(row == 2 * place, high, first)
+            both = jnp.where(row == 2 * place, high, jnp.where(row == 2 * place + 1, vector - high, both))
+        left = jnp.concatenate([both, first], axis=1).astype(BF16)
+        parts = matrices[one : one + 2]
+        axis = 1 if flipped else 0
+        right = jnp.concatenate([jnp.concatenate([part[0], part[1]], axis=axis) for part in parts], axis=1 - axis)
+        out = lax.dot_general(left, right, (((1,), (axis,)), ((), ())), preferred_element_type=F32)
+        for place in range(len(parts)):
+            mine = out[:, place * LANES : (place + 1) * LANES]
+            results.append(mine[2 * place : 2 * place + 1] + mine[2 * place + 1 : 2 * place + 2])
+    return results
 
 
 def up_kernel(
-    offsets, rows, me_ref, mine_ref, recv_ref, table_ref, edge_ref, sigma_ref, dif_ref, m1, flipped, m3,
-    s3_ref, keep_ref, q, edges, pairs, spectrum, columns,
+    offsets, rows, me_ref, mine_ref, recv_ref, table_ref, edge_ref, sigma_ref, dif_ref, m1, m2, m3,
+    s3_ref, keep_ref, q, edges, pairs, spectrum,
 ):
     waves, nodes = m1.shape[:2]
     count = len(offsets)
@@ -237,69 +290,72 @@
     residual = []
     for t in range(count):
         prev, succ = (t - 1) % count, (t + 1) % count
-        residual.append(last_of(prev, 0) - lam * first_of(t, 0) + 0.5 * first_of(t, 2) * last_of(prev, 1))
-        residual.append(first_of(succ, 0) - lam * last_of(t, 0) - 0.5 * last_of(t, 2) * first_of(succ, 1))
+        residual.append(last_of(prev, 0) - lam * first_of(t, 0) + 0.5 * first_of(t, 1) * last_of(prev, 2))
+        residual.append(first_of(succ, 0) - lam * last_of(t, 0) - 0.5 * last_of(t, 1) * first_of(succ, 2))
 
     def edge_step(wave, carry):
-        total = edge_ref[wave, 0] * residual[0]
+        total = edge_ref[wave, pl.ds(0, 1), :] * residual[0]
         for place in range(1, 2 * count):
-            total = total + edge_ref[wave, place] * residual[place]
-        leaf = total / (dif + sigma_ref[wave])
+            total = total + edge_ref[wave, pl.ds(place, 1), :] * residual[place]
+        leaf = total / (dif + sigma_ref[pl.ds(wave, 1), :])
         pairs[wave] = leaf + pltpu.roll(leaf, SUB - 1, 0)
         return carry
 
-    lax.fori_loop(0, waves, edge_step, 0, unroll=2)
-    columns[...] = jnp.zeros((LANES, LANES), F32)
-    lane = lax.broadcasted_iota(jnp.int32, (LANES, LANES), 1)
-
-    def wave_step(wave, carry):
-        sums = []
-        for node in range(nodes):
-            leaf = spectrum[node, pl.ds(wave, 1), :] + pairs[wave, pl.ds(2 * node, 1), :]
-            matrix = m1[wave, node]
-            first = over_lanes(matrix, leaf)
-            keep_ref[wave, pl.ds(node, 1), :] = over_rows(matrix, first)
-            sums.append(first)
-        total = None
-        for node in range(nodes // 2):
-            second = over_rows(flipped[wave, node], sums[2 * node] + sums[2 * node + 1])
-            keep_ref[wave, pl.ds(nodes + node, 1), :] = second
-            total = second if total is None else total + second
-        third = over_lanes(m3[wave, 0], total)
-        columns[...] = jnp.where(lane == wave, third, columns[...])
+    lax.fori_loop(0, waves, edge_step, 0, unroll=4)
+    group = math.gcd(waves, GROUP)
+
+    def group_step(index, carry):
+        own = [index * group + inner for inner in range(group)]
+        level = [
+            spectrum[node, pl.ds(wave, 1), :] + pairs[wave, pl.ds(2 * node, 1), :]
+            for wave in own
+            for node in range(nodes)
+        ]
+        at = 0
+        for matrices in (m1, m2, m3):
+            here = [(wave, node) for wave in own for node in range(matrices.shape[1])]
+            level = matvecs(level, [matrices[place] for place in here], True)
+            for (wave, node), vector in zip(here, level):
+                keep_ref[wave, pl.ds(at + node, 1), :] = vector
+            at += matrices.shape[1]
+            if matrices.shape[1] > 1:
+                level = [level[2 * pair] + level[2 * pair + 1] for pair in range(len(level) // 2)]
+        for wave, vector in zip(own, level):
+            s3_ref[pl.ds(wave, 1), :] = vector
         return carry
 
-    lax.fori_loop(0, waves, wave_step, 0, unroll=2)
-    s3_ref[...] = jnp.transpose(columns[...])[: s3_ref.shape[0]]
-
-
-def down_kernel(s3_ref, other_ref, keep_ref, m1, flipped, m3, root, out_ref, lowered):
+    lax.fori_loop(0, waves // group, group_step, 0)
+
+
+def down_kernel(s3_ref, other_ref, keep_ref, m1, m2, m3, root, out_ref):
     waves, nodes = m1.shape[:2]
-    lowered[...] = jnp.zeros((LANES, LANES), F32)
     if out_ref.shape[1] > waves:
         out_ref[...] = jnp.zeros(out_ref.shape, F32)
-
-    def root_step(wave, carry):
-        own = s3_ref[pl.ds(wave, 1), :]
-        top = over_lanes(root[wave, 0], own + other_ref[pl.ds(wave, 1), :])
-        lowered[pl.ds(wave, 1), :] = own - over_rows(root[wave, 0], top)
+    group = math.gcd(waves, GROUP)
+
+    def group_step(index, carry):
+        own = [index * group + inner for inner in range(group)]
+        roots = [root[wave, 0] for wave in own]
+        level = [s3_ref[pl.ds(wave, 1), :] for wave in own]
+        top = matvecs([value + other_ref[pl.ds(wave, 1), :] for wave, value in zip(own, level)], roots, True)
+        level = [value - back for value, back in zip(level, matvecs(top, roots, False))]
+        at = nodes + nodes // 2
+        for matrices in (m3, m2, m1):
+            here = [(wave, node) for wave in own for node in range(matrices.shape[1])]
+            level = matvecs(level, [matrices[place] for place in here], False)
+            if matrices.shape[1] < nodes:
+                below = 2 * matrices.shape[1]
+                at -= below
+                level = [
+                    keep_ref[wave, pl.ds(at + 2 * node + child, 1), :] - vector
+                    for (wave, node), vector in zip(here, level)
+                    for child in range(2)
+                ]
+        for (wave, node), vector in zip(here, level):
+            out_ref[node, pl.ds(wave, 1), :] = vector
         return carry
 
-    lax.fori_loop(0, waves, root_step, 0, unroll=4)
-    lowered[...] = jnp.transpose(lowered[...])
-    lane = lax.broadcasted_iota(jnp.int32, (LANES, LANES), 1)
-
-    def wave_step(wave, carry):
-        third = jnp.sum(jnp.where(lane == wave, lowered[...], 0.0), axis=1, keepdims=True)
-        third = over_rows(m3[wave, 0], third)
-        for pair in range(nodes // 2):
-            second = over_lanes(flipped[wave, pair], keep_ref[wave, pl.ds(nodes + pair, 1), :] - third)
-            for node in (2 * pair, 2 * pair + 1):
-                first = keep_ref[wave, pl.ds(node, 1), :] - over_rows(m1[wave, node], second)
-                out_ref[node, pl.ds(wave, 1), :] = first
-        return carry
-
-    lax.fori_loop(0, waves, wave_step, 0, unroll=2)
+    lax.fori_loop(0, waves // group, group_step, 0)
 
 
 def change_of(pairs, count, mine_ref, recv_ref, table_ref, waves):
@@ -362,9 +418,9 @@
     change[...] = change_of(range(domains // 2), count, mine_ref, recv_ref, table_ref, waves)
 
     def step(block, carry):
-        column = pl.multiple_of((block // per_pair) * LANES, LANES)
+        at = column(block // per_pair)
         value, outer = pressure_block(
-            planes, block, change[:, pl.ds(column, LANES)], q_ref, inflow_ref, diag_ref, inv_ref
+            planes, block, change[:, pl.ds(at, LANES)], q_ref, inflow_ref, diag_ref, inv_ref
         )
         here = pl.multiple_of((block + 1) * LANES, LANES)
         ext[pl.ds(SUB, rows), pl.ds(here, LANES)] = value
@@ -387,7 +443,7 @@
     def step(block, carry):
         start = pl.multiple_of(block * LANES, LANES)
         sv = sv_ref[:, pl.ds(start, LANES)]
-        _, total = convection(ext, block, nblocks, rows, sv, fw_ref, nb_ref)
+        _, total = convection(ext, block + 1, block, nblocks, rows, sv, fw_ref, nb_ref)
         out_ref[:, pl.ds(start, LANES)] = v_ref[:, pl.ds(start, LANES)] - total
         return carry
 
@@ -402,17 +458,18 @@
     return pltpu.with_memory_space_constraint(value, pltpu.HBM)
 
 
-PARAMS = pltpu.CompilerParams(vmem_limit_bytes=40 * 1024 * 1024)
-
-
-def call(kernel, outs, args, scratch=(), specs=None, out_specs=None):
+MEBI = 1024 * 1024
+
+
+def call(kernel, outs, args, scratch=(), specs=None, out_specs=None, aliases=None, limit=8):
     return pl.pallas_call(
         kernel,
         out_shape=[jax.ShapeDtypeStruct(*out) for out in outs],
         in_specs=specs or whole(*args),
         out_specs=out_specs or whole(*outs),
         scratch_shapes=list(scratch),
-        compiler_params=PARAMS,
+        compiler_params=pltpu.CompilerParams(vmem_limit_bytes=limit * MEBI),
+        input_output_aliases=aliases or {},
     )(*(in_hbm(arg) if spec is HBM else arg for arg, spec in zip(args, specs or whole(*args))))
 
 
@@ -477,13 +534,15 @@
     block_rows = 2 * rows + 3 * SUB
     vmem = pl.BlockSpec(memory_space=pltpu.VMEM)
     smem = pl.BlockSpec(memory_space=pltpu.SMEM)
-    payload, local, edge, dif, field_in, sv_in, fw_in, nb_in, diag_in, iface_in = call(
+    ext_shape = (rows + 2 * SUB, cells + 2 * LANES)
+    across = boundary(field)
+    local, edge, strip, extended, field_in, sv_in, fw_in, nb_in, diag_in, iface_in = call(
         functools.partial(source_kernel, planes),
         [
-            ((block_rows, 2 * LANES), F32),
             ((rows, cells), F32),
             ((6, nblocks, LANES), F32),
-            ((domains, LANES), F32),
+            ((SUB, cells), F32),
+            (ext_shape, F32),
             ((rows, cells), F32),
             ((rows, cells), F32),
             (flux_weight.shape, F32),
@@ -491,63 +550,82 @@
             ((nblocks, LANES), F32),
             (interface.shape, jnp.int32),
         ],
-        (boundary(field), field, sv, flux_weight, neighbours, diag, interface),
+        (field, sv, flux_weight, neighbours, diag, interface),
+        [pltpu.SemaphoreType.DMA((6,))],
+        [HBM] * 6,
+    )
+    local, edge, strip, payload, dif = call(
+        functools.partial(seam_kernel, planes),
         [
-            pltpu.VMEM((rows + 2 * SUB, cells + 2 * LANES), F32),
-            pltpu.VMEM((SUB, cells), F32),
-            pltpu.SemaphoreType.DMA((6,)),
+            ((rows, cells), F32),
+            ((6, nblocks, LANES), F32),
+            ((SUB, cells), F32),
+            ((block_rows, 2 * LANES), F32),
+            ((domains, LANES), F32),
         ],
-        [vmem] + [HBM] * 6,
+        (dom.reshape(1), across, local, edge, strip, extended, sv_in, fw_in, nb_in, diag_in, iface_in),
+        [pltpu.VMEM((rows + 2 * SUB, 3 * LANES), F32)],
+        [smem] + [vmem] * 10,
+        aliases={2: 0, 3: 1, 4: 2},
     )
     mine, received = gathered(payload, "span")
 
-    slot_of, m1, flipped, m3, root = call(
+    in_parts = lambda value: (value.shape[:2] + (2,) + value.shape[2:], BF16)
+    slot_of, m1, m2, m3, root = call(
         stage_kernel,
         [
             ((nblocks, LANES), jnp.int32),
-            (schur_one.shape, F32),
-            (schur_two.shape, F32),
-            (schur_three.shape, F32),
-            (schur_root.shape, F32),
+            in_parts(schur_one),
+            in_parts(schur_two),
+            in_parts(schur_three),
+            in_parts(schur_root),
         ],
         (iface_in, schur_one, schur_two, schur_three, schur_root),
-        [pltpu.VMEM(schur_two.shape, F32), pltpu.SemaphoreType.DMA((4,))],
+        [pltpu.VMEM(value.shape, F32) for value in (schur_one, schur_two, schur_three, schur_root)]
+        + [pltpu.SemaphoreType.DMA((7,))],
         [vmem] + [HBM] * 4,
+        limit=24,
     )
     own_wave = me * waves + jnp.arange(waves, dtype=jnp.int32)
-    xored = me ^ jnp.array(offsets, jnp.int32)
+    order = jnp.arange(count, dtype=jnp.int32)
+    xored = me ^ (2 * (order % (count // 2)) + order // (count // 2))
     plane_of = xored[:, None] * planes + jnp.arange(rows, dtype=jnp.int32)[None, :]
     valid = jnp.arange(rows) < planes
     table = jnp.where(valid[None, None], fourier_entry(own_wave[:, None, None], plane_of[None]), 0.0)
     table = jnp.pad(table.reshape(waves, count * rows), ((0, wave_rows - waves), (0, 0)))
     edge_planes = (jnp.arange(count)[:, None] * planes + jnp.array([0, planes - 1])[None, :]).reshape(-1)
     edge_table = fourier_entry(own_wave[:, None], edge_planes[None, :].astype(jnp.int32))
-    sigma = wave_shift(own_wave)
+    edge_table = jnp.broadcast_to(edge_table[:, :, None], edge_table.shape + (LANES,))
+    sigma = jnp.broadcast_to(wave_shift(own_wave)[:, None], (waves, LANES))
+    wave_of = xored[:, None] * waves + jnp.arange(wave_rows, dtype=jnp.int32)[None, :]
+    row_ids = jnp.arange(rows + SUB, dtype=jnp.int32)
+    row_plane = jnp.where(row_ids < rows, row_ids, jnp.where(row_ids == rows, -1, planes))
+    row_plane = (me * planes + row_plane + PLANES) % PLANES
+    back_table = fourier_entry(wave_of[None], row_plane[:, None, None])
+    back_table = jnp.where((jnp.arange(wave_rows) < waves)[None, None], back_table, 0.0)
+    back_table = back_table.reshape(rows + SUB, count * wave_rows)
     s3, keep = call(
         functools.partial(up_kernel, offsets, rows),
         [((wave_rows, LANES), F32), ((waves, SUB, LANES), F32)],
-        (me.reshape(1), mine, received, table, edge_table, sigma, dif, m1, flipped, m3),
+        (me.reshape(1), mine, received, table, edge_table, sigma, dif, m1, m2, m3),
         [
             pltpu.VMEM((count * rows, pair_cells), F32),
             pltpu.VMEM((count, 3 * SUB, 2 * LANES), F32),
             pltpu.VMEM((waves, SUB, LANES), F32),
             pltpu.VMEM((pair_cells // LANES, wave_rows, LANES), F32),
-            pltpu.VMEM((LANES, LANES), F32),
         ],
-        [smem, vmem, vmem, vmem, smem, smem] + [vmem] * 4,
+        [smem] + [vmem] * 9,
+        limit=16,
     )
     other = xor_permute(s3, "dom", 1)
     (returned,) = call(
-        down_kernel,
-        [((pair_cells // LANES, wave_rows, LANES), F32)],
-        (s3, other, keep, m1, flipped, m3, root),
-        [pltpu.VMEM((LANES, LANES), F32)],
+        down_kernel, [((pair_cells // LANES, wave_rows, LANES), F32)], (s3, other, keep, m1, m2, m3, root), limit=16
     )
     mine, received = gathered(returned.reshape(-1, LANES), "span")
 
     up_ring = [(i, (i + 1) % count) for i in range(count)]
     down_ring = [(j, i) for i, j in up_ring]
-    q_first, q_last, v_first, v_last, sv_first, sv_last = (edge[i] for i in range(6))
+    q_first, q_last, sv_first, sv_last, v_first, v_last = (edge[i] for i in range(6))
     lam, kappa = decay(diag_in)
     v_before, v_after = lax.ppermute(v_last, "span", up_ring), lax.ppermute(v_first, "span", down_ring)
     at_first = kappa * 0.5 * sv_first * v_before
@@ -562,13 +640,6 @@
     left, right = inflow(ends, diag_in, planes)
     flows = jnp.stack([left, right, at_first, at_last])
 
-    wave_of = xored[:, None] * waves + jnp.arange(wave_rows, dtype=jnp.int32)[None, :]
-    row_ids = jnp.arange(rows + SUB, dtype=jnp.int32)
-    row_plane = jnp.where(row_ids < rows, row_ids, jnp.where(row_ids == rows, -1, planes))
-    row_plane = (me * planes + row_plane + PLANES) % PLANES
-    back_table = fourier_entry(wave_of[None], row_plane[:, None, None])
-    back_table = jnp.where((jnp.arange(wave_rows) < waves)[None, None], back_table, 0.0)
-    back_table = back_table.reshape(rows + SUB, count * wave_rows)
     wave_scratch = lambda pairs: pltpu.VMEM((count * wave_rows, pairs * LANES), F32)
     parts = (mine, received, back_table, local, flows, diag_in, slot_of)
     (rim,) = call(
@@ -579,7 +650,6 @@
         [smem] + [vmem] * 7,
     )
     halo = xor_permute(rim, "dom", 1)
-    ext_shape = (rows + 2 * SUB, cells + 2 * LANES)
     (extended,) = call(
         functools.partial(pressure_kernel, planes, domains, count),
         [(ext_shape, F32)],

time: 52 us -> 53.3 us (1.025)
  waiting for transfers between devices: 14.6 us -> 18.1 us
  Pallas kernels: 16.7 us -> 14.7 us
  other arithmetic: 2.16 us -> 1.5 us
    pallas_call x7 -> x8, Pallas kernels: 16.7 us -> 14.7 us  [call(): pl.pallas_call(kernel, out_shape=[jax.ShapeDtypeStruct(*out) for out in o...]
    ppermute x14, waiting for transfers between devices: 14.6 us -> 16.6 us  [xor_permute(): lax.ppermute(value, axis, [(i, i ^ mask) for i in range(lax.axis_size(axi...]
    ppermute x1, waiting for transfers between devices: 0.01 us -> 1.5 us  [on_device(): lax.ppermute(v_last, 'span', up_ring)]
    mul x1, other arithmetic: 0.66 us -> 0.01 us  [on_device(): xored[:, None] * planes + jnp.arange(rows, dtype=jnp.int32)[None, :]]
  transfers between devices with their start and end apart: 16 -> 16, of which waited for: 10 -> 10; matrix products, arithmetic and copies ran while one was open for 4% -> 2% of each run, Pallas kernels for 16% -> 19%
where the time goes in v1:
time: 53.3 us; the launch traced here: 53.1 us
  waiting for transfers between devices  18.1 us (34%)
  starting transfers between devices  17.3 us (32%)
  Pallas kernels  14.7 us (28%)
  other arithmetic  1.5 us (3%)
  between operations  0.94 us (2%)
  local copies, waits for them, and re-layouts  0.59 us (1%)
    ppermute x14, waiting for transfers between devices, xor_permute(): lax.ppermute(value, axis, [(i, i ^ mask) for i in range(lax.axis_size(axi...  16.6 us
    pallas_call x8, Pallas kernels, call(): pl.pallas_call(kernel, out_shape=[jax.ShapeDtypeStruct(*out) for out in o...  14.7 us
    ppermute x14, starting transfers between devices, xor_permute(): lax.ppermute(value, axis, [(i, i ^ mask) for i in range(lax.axis_size(axi...  11.6 us
    ppermute x1, starting transfers between devices, on_device(): lax.ppermute(v_first, 'span', down_ring)  3.1 us
    ppermute x1, starting transfers between devices, on_device(): lax.ppermute(v_last, 'span', up_ring)  2.56 us
    ppermute x1, waiting for transfers between devices, on_device(): lax.ppermute(v_last, 'span', up_ring)  1.5 us
  transfers between devices with their start and end apart: 16, of which 10 were waited for; matrix products, arithmetic and copies ran while one was open for 2% of the time, Pallas kernels for 19%

profile of v1, /device:TPU:0, one launch (start us, length us, event | category | flops | bytes accessed | tf_op | source)
XLA Modules:
  0.0 53.1 jit_solution(2163933969113226909)
XLA Ops:
  0.6 0.7 %slice_select_fusion = f32[16,128]{1,0:T(8,128)S(1)} fusion(f32[16,4096]{1,0:T(8,128)} %v_hbm.1, pred[]{:T(512)S(6)} %eq.97), kind=kLoop, calls=%fused_computation.88 | loop fusion | flops 2048 | bytes 24577 | tf_op jit(solution)/shard_map/jit(_where)/select_n | solution.py:531
  1.4 0.5 collective-permute-start
  2.3 0.1 broadcast_in_dim.118
  2.3 0.1 multiply_select_fusion.7.table_ref
  2.5 0.1 multiply_select_fusion.6.table_ref
  2.6 2.8 %shard_map.122 = (f32[16,4096]{1,0:T(8,128)S(1)}, f32[6,32,128]{2,1,0:T(8,128)S(1)}, f32[8,4096]{1,0:T(8,128)S(1)}, f32[32,4352]{1,0:T(8,128)S(1)}, f32[16,4096]...) custom-call(f32[16,4096]{1,0:T(8,128)} %v_hbm.1, ...), custom_call_target="tpu_custom_call" | custom-call | tf_op jit(solution)/shard_map/pallas_call | solution.py:465
  5.5 0.3 shard_map.123
  5.8 2.6 %collective-permute-start.10 = (f32[32,128]{1,0:T(8,128)S(1)}, f32[32,128]{1,0:T(8,128)S(1)}, u32[]{:S(2)}, u32[]{:S(2)}) collective-permute-start(f32[32,128]{1,0:T(8,128)S(1)} %get-tuple-element.52), channel_id=1, source_target_pairs={{0,2},{2,4},{4,6},{6,8},{8,10},{10,12},{12,14},{14,0},{1,3},{3,5},... | collective-permute-start | bytes 49160 | tf_op jit(solution)/shard_map/ppermute | solution.py:630
  8.4 3.1 %collective-permute-start.11 = (f32[32,128]{1,0:T(8,128)S(1)}, f32[32,128]{1,0:T(8,128)S(1)}, u32[]{:S(2)}, u32[]{:S(2)}) collective-permute-start(f32[32,128]{1,0:T(8,128)S(1)} %get-tuple-element.51), channel_id=1, source_target_pairs={{2,0},{4,2},{6,4},{8,6},{10,8},{12,10},{14,12},{0,14},{3,1},{5,3},... | collective-permute-start | bytes 49160 | tf_op jit(solution)/shard_map/ppermute | solution.py:630
  11.6 1.5 %collective-permute-done.10 = f32[32,128]{1,0:T(8,128)S(1)} collective-permute-done((f32[32,128]{1,0:T(8,128)S(1)}, f32[32,128]{1,0:T(8,128)S(1)}, u32[]{:S(2)}, u32[]{:S(2)}) %collective-permute-start.10) | collective-permute-done | bytes 16416 | tf_op jit(solution)/shard_map/ppermute | solution.py:630
  13.2 1.5 %collective-permute-start.12 = (f32[2,32,128]{2,1,0:T(8,128)S(1)}, f32[2,32,128]{2,1,0:T(8,128)S(1)}, u32[]{:S(2)}, u32[]{:S(2)}) collective-permute-start(f32[2,32,128]{2,1,0:T(8,128)S(1)} %pad_maximum_fusion.2), channel_id=1, source_target_pairs={{0,2},{2,0},{4,6},{6,4},{8,10},{10,8},{12,14},{14,12},{1,3},{3,1},... | collective-permute-start | bytes 98312 | tf_op jit(solution)/shard_map/ppermute | solution.py:38
  14.7 1.6 %collective-permute-start.1 = (f32[56,256]{1,0:T(8,128)S(1)}, f32[56,256]{1,0:T(8,128)S(1)}, u32[]{:S(2)}, u32[]{:S(2)}) collective-permute-start(f32[56,256]{1,0:T(8,128)S(1)} %get-tuple-element.32), channel_id=1, source_target_pairs={{0,4},{2,6},{4,0},{6,2},{8,12},{10,14},{12,8},{14,10},{1,5},{3,7},... | collective-permute-start | bytes 172040 | tf_op jit(solution)/shard_map/ppermute | solution.py:38
  16.3 2.9 %collective-permute-start.2 = (f32[56,256]{1,0:T(8,128)S(1)}, f32[56,256]{1,0:T(8,128)S(1)}, u32[]{:S(2)}, u32[]{:S(2)}) collective-permute-start(f32[56,256]{1,0:T(8,128)S(1)} %get-tuple-element.32), channel_id=1, source_target_pairs={{0,8},{2,10},{4,12},{6,14},{8,0},{10,2},{12,4},{14,6},{1,9},{3,11}... | collective-permute-start | bytes 172040 | tf_op jit(solution)/shard_map/ppermute | solution.py:38
  19.3 2.7 %collective-permute-done.2 = f32[56,256]{1,0:T(8,128)S(1)} collective-permute-done((f32[56,256]{1,0:T(8,128)S(1)}, f32[56,256]{1,0:T(8,128)S(1)}, u32[]{:S(2)}, u32[]{:S(2)}) %collective-permute-start.2) | collective-permute-done | bytes 57376 | tf_op jit(solution)/shard_map/ppermute | solution.py:38
  22.0 3.6 %collective-permute-done.3 = f32[56,256]{1,0:T(8,128)S(1)} collective-permute-done((f32[56,256]{1,0:T(8,128)S(1)}, f32[56,256]{1,0:T(8,128)S(1)}, u32[]{:S(2)}, u32[]{:S(2)}) %collective-permute-start.3) | collective-permute-done | bytes 57376 | tf_op jit(solution)/shard_map/ppermute | solution.py:38
  25.6 0.1 select_multiply_fusion
  25.8 3.6 %shard_map.124 = (s32[32,128]{1,0:T(8,128)S(1)}, bf16[16,4,2,128,128]{4,3,2,1,0:T(8,128)(2,1)S(1)}, bf16[16,2,2,128,128]{4,3,2,1,0:T(8,128)(2,1)S(1)}, bf16[16,1...) custom-call(s32[8,128]{1,0:T(8,128)S(1)} %get-tuple-element.31.iface_ref, f32[16,4,128,128]{3,2,1,0:T(8,128)} %m1_hbm.1, ...), custom_call_target="tpu_custom_call" | custom-call | tf_op jit(solution)/shard_map/pallas_call | solution.py:465
  29.4 2.2 %collective-permute-done.4.recv_ref = f32[224,256]{1,0:T(8,128)S(1)} collective-permute-done((f32[224,256]{1,0:T(8,128)S(1)}, f32[224,256]{1,0:T(8,128)S(1)}, u32[]{:S(2)}, u32[]{:S(2)}) %collective-permute-start.4) | collective-permute-done | bytes 229408 | tf_op jit(solution)/shard_map/ppermute | solution.py:38
  31.7 2.5 %shard_map.125 = (f32[16,128]{1,0:T(8,128)S(1)}, f32[16,8,128]{2,1,0:T(8,128)S(1)}) custom-call(s32[1]{0:T(128)} %bitcast.me_ref, f32[224,256]{1,0:T(8,128)S(1)} %constant_dynamic-update-slice_fusion.mine_ref, f32[224,256]{1,0:T(8,128)S(1)} %collective-permute-done.4.recv_ref, f32[16,128]{1,0:T(8,128)S(1)} %multiply_select_fusion.7.table_ref, ...), custom_call_target="tpu_custom_call" | custom-call | tf_op jit(solution)/shard_map/pallas_call | solution.py:465
  34.4 1.1 %collective-permute-done.5.other_ref = f32[16,128]{1,0:T(8,128)S(1)} collective-permute-done((f32[16,128]{1,0:T(8,128)S(1)}, f32[16,128]{1,0:T(8,128)S(1)}, u32[]{:S(2)}, u32[]{:S(2)}) %collective-permute-start.5) | collective-permute-done | bytes 8224 | tf_op jit(solution)/shard_map/ppermute | solution.py:38
  35.5 1.9 %shard_map.126 = f32[4,16,128]{2,1,0:T(8,128)S(1)} custom-call(f32[16,128]{1,0:T(8,128)S(1)} %get-tuple-element.37.s3_ref, f32[16,128]{1,0:T(8,128)S(1)} %collective-permute-done.5.other_ref, f32[16,8,128]{2,1,0:T(8,128)S(1)} %get-tuple-element.38.keep_ref, bf16[16,4,2,128,128]{4,3,2,1,0:T(8,128)(2,1)S(1)} %get-tuple-element.34.m1, ...), custom_call_target="tpu_custom_call" | custom-call | tf_op jit(solution)/shard_map/pallas_call | solution.py:465
  37.4 0.9 %collective-permute-start.7 = (f32[64,128]{1,0:T(8,128)S(1)}, f32[64,128]{1,0:T(8,128)S(1)}, u32[]{:S(2)}, u32[]{:S(2)}) collective-permute-start(f32[64,128]{1,0:T(8,128)S(1)} %bitcast.83), channel_id=1, source_target_pairs={{0,8},{2,10},{4,12},{6,14},{8,0},{10,2},{12,4},{14,6},{1,9},{3,11}... | collective-permute-start | bytes 98312 | tf_op jit(solution)/shard_map/ppermute | solution.py:38
  38.3 3.5 %collective-permute-start.8 = (f32[64,128]{1,0:T(8,128)S(1)}, f32[64,128]{1,0:T(8,128)S(1)}, u32[]{:S(2)}, u32[]{:S(2)}) collective-permute-start(f32[64,128]{1,0:T(8,128)S(1)} %bitcast.84), channel_id=1, source_target_pairs={{0,12},{2,14},{4,8},{6,10},{8,4},{10,6},{12,0},{14,2},{1,13},{3,15... | collective-permute-start | bytes 98312 | tf_op jit(solution)/shard_map/ppermute | solution.py:38
  41.8 0.5 collective-permute-done.7
  42.3 2.1 %collective-permute-done.8 = f32[64,128]{1,0:T(8,128)S(1)} collective-permute-done((f32[64,128]{1,0:T(8,128)S(1)}, f32[64,128]{1,0:T(8,128)S(1)}, u32[]{:S(2)}, u32[]{:S(2)}) %collective-permute-start.8) | collective-permute-done | bytes 32800 | tf_op jit(solution)/shard_map/ppermute | solution.py:38
  44.4 0.6 %collective-permute-start.9 = (f32[256,128]{1,0:T(8,128)S(1)}, f32[256,128]{1,0:T(8,128)S(1)}, u32[]{:S(2)}, u32[]{:S(2)}) collective-permute-start(f32[256,128]{1,0:T(8,128)S(1)} %pad_maximum_fusion.mine_ref), channel_id=1, source_target_pairs={{0,2},{2,0},{4,6},{6,4},{8,10},{10,8},{12,14},{14,12},{1,3},{3,1},... | collective-permute-start | bytes 393224 | tf_op jit(solution)/shard_map/ppermute | solution.py:38
  45.0 1.6 %collective-permute-done.14 = f32[2,32,128]{2,1,0:T(8,128)S(1)} collective-permute-done((f32[2,32,128]{2,1,0:T(8,128)S(1)}, f32[2,32,128]{2,1,0:T(8,128)S(1)}, u32[]{:S(2)}, u32[]{:S(2)}) %collective-permute-start.14) | collective-permute-done | bytes 32800 | tf_op jit(solution)/shard_map/ppermute | solution.py:38
  46.6 2.8 %collective-permute-done.9.recv_ref = f32[256,128]{1,0:T(8,128)S(1)} collective-permute-done((f32[256,128]{1,0:T(8,128)S(1)}, f32[256,128]{1,0:T(8,128)S(1)}, u32[]{:S(2)}, u32[]{:S(2)}) %collective-permute-start.9) | collective-permute-done | bytes 131104 | tf_op jit(solution)/shard_map/ppermute | solution.py:38
  49.4 0.2 shard_map.128
  49.7 1.1 %shard_map.127.ext_in = f32[32,4352]{1,0:T(8,128)S(1)} custom-call(f32[256,128]{1,0:T(8,128)S(1)} %pad_maximum_fusion.mine_ref, f32[256,128]{1,0:T(8,128)S(1)} %collective-permute-done.9.recv_ref, f32[24,128]{1,0:T(8,128)S(1)} %multiply_select_fusion.6.table_ref, f32[16,4096]{1,0:T(8,128)S(1)} %get-tuple-element.40.q_ref, ...), custom_call_target="tpu_custom_call" | custom-call | tf_op jit(solution)/shard_map/pallas_call | solution.py:465
  50.7 0.1 collective-permute-done.15.halo_ref
  50.8 2.3 %shard_map.129 = (f32[16,4096]{1,0:T(8,128)}, f32[16,4096]{1,0:T(8,128)}) custom-call(f32[32,4352]{1,0:T(8,128)S(1)} %shard_map.127.ext_in, f32[16,4096]{1,0:T(8,128)S(1)} %get-tuple-element.43.v_ref, f32[16,128]{1,0:T(8,128)S(1)} %collective-permute-done.15.halo_ref, f32[16,4096]{1,0:T(8,128)S(1)} %get-tuple-element.27.sv_ref, ...), custom_call_target="tpu_custom_call" | custom-call | tf_op jit(solution)/shard_map/pallas_call | solution.py:465
  (48 shorter events, 1.1 us)
Async XLA Ops:
  1.4 4.1 %collective-permute-start = (f32[16,128]{1,0:T(8,128)S(1)}, f32[16,128]{1,0:T(8,128)S(1)}, u32[]{:S(2)}, u32[]{:S(2)}) collective-permute-start(f32[16,128]{1,0:T(8,128)S(1)} %slice_select_fusion), channel_id=1, source_target_pairs={{0,1},{1,0},{2,3},{3,2},{4,5},{5,4},{6,7},{7,6},{8,9},{9,8},{10,11... | collective-permute-start | bytes 24584 | tf_op jit(solution)/shard_map/ppermute | solution.py:38
  5.8 7.3 %collective-permute-start.10 = (f32[32,128]{1,0:T(8,128)S(1)}, f32[32,128]{1,0:T(8,128)S(1)}, u32[]{:S(2)}, u32[]{:S(2)}) collective-permute-start(f32[32,128]{1,0:T(8,128)S(1)} %get-tuple-element.52), channel_id=1, source_target_pairs={{0,2},{2,4},{4,6},{6,8},{8,10},{10,12},{12,14},{14,0},{1,3},{3,5},... | collective-permute-start | bytes 49160 | tf_op jit(solution)/shard_map/ppermute | solution.py:630
  8.4 4.8 %collective-permute-start.11 = (f32[32,128]{1,0:T(8,128)S(1)}, f32[32,128]{1,0:T(8,128)S(1)}, u32[]{:S(2)}, u32[]{:S(2)}) collective-permute-start(f32[32,128]{1,0:T(8,128)S(1)} %get-tuple-element.51), channel_id=1, source_target_pairs={{2,0},{4,2},{6,4},{8,6},{10,8},{12,10},{14,12},{0,14},{3,1},{5,3},... | collective-permute-start | bytes 49160 | tf_op jit(solution)/shard_map/ppermute | solution.py:630
  13.2 6.0 %collective-permute-start.12 = (f32[2,32,128]{2,1,0:T(8,128)S(1)}, f32[2,32,128]{2,1,0:T(8,128)S(1)}, u32[]{:S(2)}, u32[]{:S(2)}) collective-permute-start(f32[2,32,128]{2,1,0:T(8,128)S(1)} %pad_maximum_fusion.2), channel_id=1, source_target_pairs={{0,2},{2,0},{4,6},{6,4},{8,10},{10,8},{12,14},{14,12},{1,3},{3,1},... | collective-permute-start | bytes 98312 | tf_op jit(solution)/shard_map/ppermute | solution.py:38
  14.7 4.6 %collective-permute-start.1 = (f32[56,256]{1,0:T(8,128)S(1)}, f32[56,256]{1,0:T(8,128)S(1)}, u32[]{:S(2)}, u32[]{:S(2)}) collective-permute-start(f32[56,256]{1,0:T(8,128)S(1)} %get-tuple-element.32), channel_id=1, source_target_pairs={{0,4},{2,6},{4,0},{6,2},{8,12},{10,14},{12,8},{14,10},{1,5},{3,7},... | collective-permute-start | bytes 172040 | tf_op jit(solution)/shard_map/ppermute | solution.py:38
  16.3 5.7 %collective-permute-start.2 = (f32[56,256]{1,0:T(8,128)S(1)}, f32[56,256]{1,0:T(8,128)S(1)}, u32[]{:S(2)}, u32[]{:S(2)}) collective-permute-start(f32[56,256]{1,0:T(8,128)S(1)} %get-tuple-element.32), channel_id=1, source_target_pairs={{0,8},{2,10},{4,12},{6,14},{8,0},{10,2},{12,4},{14,6},{1,9},{3,11}... | collective-permute-start | bytes 172040 | tf_op jit(solution)/shard_map/ppermute | solution.py:38
  19.2 6.3 %collective-permute-start.3 = (f32[56,256]{1,0:T(8,128)S(1)}, f32[56,256]{1,0:T(8,128)S(1)}, u32[]{:S(2)}, u32[]{:S(2)}) collective-permute-start(f32[56,256]{1,0:T(8,128)S(1)} %get-tuple-element.32), channel_id=1, source_target_pairs={{0,12},{2,14},{4,8},{6,10},{8,4},{10,6},{12,0},{14,2},{1,13},{3,15... | collective-permute-start | bytes 172040 | tf_op jit(solution)/shard_map/ppermute | solution.py:38
  25.5 6.0 %collective-permute-start.4 = (f32[224,256]{1,0:T(8,128)S(1)}, f32[224,256]{1,0:T(8,128)S(1)}, u32[]{:S(2)}, u32[]{:S(2)}) collective-permute-start(f32[224,256]{1,0:T(8,128)S(1)} %constant_dynamic-update-slice_fusion.mine_ref), channel_id=1, source_target_pairs={{0,2},{2,0},{4,6},{6,4},{8,10},{10,8},{12,14},{14,12},{1,3},{3,1},... | collective-permute-start | bytes 688136 | tf_op jit(solution)/shard_map/ppermute | solution.py:38
  25.6 8.7 %collective-permute-start.13 = (f32[2,32,128]{2,1,0:T(8,128)S(1)}, f32[2,32,128]{2,1,0:T(8,128)S(1)}, u32[]{:S(2)}, u32[]{:S(2)}) collective-permute-start(f32[2,32,128]{2,1,0:T(8,128)S(1)} %pad_maximum_fusion.3), channel_id=1, source_target_pairs={{0,4},{2,6},{4,0},{6,2},{8,12},{10,14},{12,8},{14,10},{1,5},{3,7},... | collective-permute-start | bytes 98312 | tf_op jit(solution)/shard_map/ppermute | solution.py:38
  34.3 1.2 %collective-permute-start.5 = (f32[16,128]{1,0:T(8,128)S(1)}, f32[16,128]{1,0:T(8,128)S(1)}, u32[]{:S(2)}, u32[]{:S(2)}) collective-permute-start(f32[16,128]{1,0:T(8,128)S(1)} %get-tuple-element.37.s3_ref), channel_id=1, source_target_pairs={{0,1},{1,0},{2,3},{3,2},{4,5},{5,4},{6,7},{7,6},{8,9},{9,8},{10,11... | collective-permute-start | bytes 24584 | tf_op jit(solution)/shard_map/ppermute | solution.py:38
  37.3 4.4 %collective-permute-start.6 = (f32[64,128]{1,0:T(8,128)S(1)}, f32[64,128]{1,0:T(8,128)S(1)}, u32[]{:S(2)}, u32[]{:S(2)}) collective-permute-start(f32[64,128]{1,0:T(8,128)S(1)} %bitcast.82), channel_id=1, source_target_pairs={{0,4},{2,6},{4,0},{6,2},{8,12},{10,14},{12,8},{14,10},{1,5},{3,7},... | collective-permute-start | bytes 98312 | tf_op jit(solution)/shard_map/ppermute | solution.py:38
  37.4 4.9 %collective-permute-start.7 = (f32[64,128]{1,0:T(8,128)S(1)}, f32[64,128]{1,0:T(8,128)S(1)}, u32[]{:S(2)}, u32[]{:S(2)}) collective-permute-start(f32[64,128]{1,0:T(8,128)S(1)} %bitcast.83), channel_id=1, source_target_pairs={{0,8},{2,10},{4,12},{6,14},{8,0},{10,2},{12,4},{14,6},{1,9},{3,11}... | collective-permute-start | bytes 98312 | tf_op jit(solution)/shard_map/ppermute | solution.py:38
  38.3 6.1 %collective-permute-start.8 = (f32[64,128]{1,0:T(8,128)S(1)}, f32[64,128]{1,0:T(8,128)S(1)}, u32[]{:S(2)}, u32[]{:S(2)}) collective-permute-start(f32[64,128]{1,0:T(8,128)S(1)} %bitcast.84), channel_id=1, source_target_pairs={{0,12},{2,14},{4,8},{6,10},{8,4},{10,6},{12,0},{14,2},{1,13},{3,15... | collective-permute-start | bytes 98312 | tf_op jit(solution)/shard_map/ppermute | solution.py:38
  41.8 4.8 %collective-permute-start.14 = (f32[2,32,128]{2,1,0:T(8,128)S(1)}, f32[2,32,128]{2,1,0:T(8,128)S(1)}, u32[]{:S(2)}, u32[]{:S(2)}) collective-permute-start(f32[2,32,128]{2,1,0:T(8,128)S(1)} %pad_maximum_fusion.4), channel_id=1, source_target_pairs={{0,8},{2,10},{4,12},{6,14},{8,0},{10,2},{12,4},{14,6},{1,9},{3,11}... | collective-permute-start | bytes 98312 | tf_op jit(solution)/shard_map/ppermute | solution.py:38
  44.4 5.0 %collective-permute-start.9 = (f32[256,128]{1,0:T(8,128)S(1)}, f32[256,128]{1,0:T(8,128)S(1)}, u32[]{:S(2)}, u32[]{:S(2)}) collective-permute-start(f32[256,128]{1,0:T(8,128)S(1)} %pad_maximum_fusion.mine_ref), channel_id=1, source_target_pairs={{0,2},{2,0},{4,6},{6,4},{8,10},{10,8},{12,14},{14,12},{1,3},{3,1},... | collective-permute-start | bytes 393224 | tf_op jit(solution)/shard_map/ppermute | solution.py:38
  49.6 1.2 %collective-permute-start.15 = (f32[16,128]{1,0:T(8,128)S(1)}, f32[16,128]{1,0:T(8,128)S(1)}, u32[]{:S(2)}, u32[]{:S(2)}) collective-permute-start(f32[16,128]{1,0:T(8,128)S(1)} %shard_map.128), channel_id=1, source_target_pairs={{0,1},{1,0},{2,3},{3,2},{4,5},{5,4},{6,7},{7,6},{8,9},{9,8},{10,11... | collective-permute-start | bytes 24584 | tf_op jit(solution)/shard_map/ppermute | solution.py:38

commit v2 on v1

--- a/solution.py
+++ b/solution.py
@@ -38,11 +38,15 @@
     return lax.ppermute(value, axis, [(i, i ^ mask) for i in range(lax.axis_size(axis))])
 
 
-def gathered(block, axis):
+def gathered(block, axis, apart=False):
     count = lax.axis_size(axis)
-    far = [xor_permute(block, axis, mask) for mask in range(count - 2, 0, -2)]
-    mine = jnp.concatenate([block] + far[::-1], axis=0)
-    return mine, xor_permute(mine, axis, 1)
+    far = [xor_permute(block, axis, mask) for mask in range(count - 2, 0, -2)][::-1]
+    if not apart:
+        mine = jnp.concatenate([block] + far, axis=0)
+        return mine, xor_permute(mine, axis, 1)
+    beside = xor_permute(block, axis, 1)
+    mine = jnp.concatenate(far, axis=0)
+    return block, mine, beside, xor_permute(mine, axis, 1)
 
 
 def xor_offsets(count):
@@ -125,24 +129,34 @@
             edge_ref[place, pl.ds(block, 1), :] = value
 
 
+def load_kernel(
+    dom_ref, v_hbm, sv_hbm, fw_hbm, nb_hbm, diag_hbm, iface_hbm,
+    edge_ref, v_ref, sv_ref, fw_ref, nb_ref, diag_ref, iface_ref, sems,
+):
+    moved = (
+        (v_hbm, v_ref), (sv_hbm, sv_ref), (fw_hbm, fw_ref), (nb_hbm, nb_ref), (diag_hbm, diag_ref), (iface_hbm, iface_ref),
+    )
+    moves = [pltpu.make_async_copy(src, dst, sems.at[i]) for i, (src, dst) in enumerate(moved)]
+    for move in moves:
+        move.start()
+    for move in moves:
+        move.wait()
+    for side, block in ((0, v_ref.shape[1] // LANES - 1), (1, 0)):
+
+        @pl.when(dom_ref[0] == side)
+        def _(block=block):
+            edge_ref[...] = v_ref[:, pl.ds(column(block), LANES)]
+
+
 def source_kernel(
-    planes, v_hbm, sv_hbm, fw_hbm, nb_hbm, diag_hbm, iface_hbm,
-    q_ref, edge_ref, strip, ext, v_ref, sv_ref, fw_ref, nb_ref, diag_ref, iface_ref, sems,
+    planes, v_ref, sv_ref, fw_ref, nb_ref, diag_ref, q_ref, edge_ref, strip, ext
 ):
     rows, cells = v_ref.shape
     nblocks = cells // LANES
-    moved = (
-        (v_hbm, v_ref), (sv_hbm, sv_ref), (fw_hbm, fw_ref), (nb_hbm, nb_ref), (diag_hbm, diag_ref), (iface_hbm, iface_ref),
-    )
-    moves = [pltpu.make_async_copy(src, dst, sems.at[i]) for i, (src, dst) in enumerate(moved)]
-    for move in moves:
-        move.start()
     ext[pl.ds(0, SUB), :] = jnp.zeros((SUB, cells + 2 * LANES), F32)
     ext[pl.ds(SUB + rows, SUB), :] = jnp.zeros((SUB, cells + 2 * LANES), F32)
     for side in (0, LANES + cells):
         ext[pl.ds(SUB, rows), pl.ds(side, LANES)] = jnp.zeros((rows, LANES), F32)
-    for move in moves:
-        move.wait()
     ext[pl.ds(SUB, rows), pl.ds(LANES, cells)] = v_ref[...]
 
     def step(block, carry):
@@ -265,7 +279,7 @@
 
 
 def up_kernel(
-    offsets, rows, me_ref, mine_ref, recv_ref, table_ref, edge_ref, sigma_ref, dif_ref, m1, m2, m3,
+    offsets, rows, me_ref, own_ref, mine_ref, beside_ref, recv_ref, table_ref, edge_ref, sigma_ref, dif_ref, m1, m2, m3,
     s3_ref, keep_ref, q, edges, pairs, spectrum,
 ):
     waves, nodes = m1.shape[:2]
@@ -273,8 +287,9 @@
     me = me_ref[0]
     block_rows = 2 * rows + 3 * SUB
     for place, offset in enumerate(offsets):
-        source = mine_ref if place < count // 2 else recv_ref
-        base = (place % (count // 2)) * block_rows
+        side, at = divmod(place, count // 2)
+        source = ((own_ref, beside_ref) if at == 0 else (mine_ref, recv_ref))[side]
+        base = max(at - 1, 0) * block_rows
         for half in range(2):
             q[pl.ds(place * rows, rows), pl.ds(half * 2 * LANES, 2 * LANES)] = source[
                 pl.ds(base + half * rows, rows), :
@@ -358,12 +373,13 @@
     lax.fori_loop(0, waves // group, group_step, 0)
 
 
-def change_of(pairs, count, mine_ref, recv_ref, table_ref, waves):
-    nodes = mine_ref.shape[0] * 2 // waves.shape[0]
+def change_of(pairs, count, blocks, table_ref, waves):
+    own_ref, mine_ref, beside_ref, recv_ref = blocks
     wave_rows = waves.shape[0] // count
     for place in range(count):
-        source = mine_ref if place < count // 2 else recv_ref
-        base = (place % (count // 2)) * nodes * wave_rows
+        side, at = divmod(place, count // 2)
+        source = ((own_ref, beside_ref) if at == 0 else (mine_ref, recv_ref))[side]
+        base = max(at - 1, 0) * own_ref.shape[0]
         for at, pair in enumerate(pairs):
             waves[pl.ds(place * wave_rows, wave_rows), pl.ds(at * LANES, LANES)] = source[
                 pl.ds(base + pair * wave_rows, wave_rows), :
@@ -396,7 +412,7 @@
 
 
 def rim_kernel(
-    planes, domains, count, dom_ref, mine_ref, recv_ref, table_ref, q_ref, inflow_ref, diag_ref, inv_ref,
+    planes, domains, count, dom_ref, own_ref, mine_ref, beside_ref, recv_ref, table_ref, q_ref, inflow_ref, diag_ref, inv_ref,
     rim_ref, waves,
 ):
     nblocks = q_ref.shape[1] // LANES
@@ -404,18 +420,18 @@
 
         @pl.when(dom_ref[0] == side)
         def _(block=block, pair=pair):
-            change = change_of((pair,), count, mine_ref, recv_ref, table_ref, waves)
+            change = change_of((pair,), count, (own_ref, mine_ref, beside_ref, recv_ref), table_ref, waves)
             rim_ref[...] = pressure_block(planes, block, change, q_ref, inflow_ref, diag_ref, inv_ref)[0]
 
 
 def pressure_kernel(
-    planes, domains, count, mine_ref, recv_ref, table_ref, q_ref, inflow_ref, diag_ref, inv_ref,
+    planes, domains, count, own_ref, mine_ref, beside_ref, recv_ref, table_ref, q_ref, inflow_ref, diag_ref, inv_ref,
     ext, change, waves,
 ):
     rows, cells = q_ref.shape
     nblocks = cells // LANES
     per_pair = 2 * nblocks // domains
-    change[...] = change_of(range(domains // 2), count, mine_ref, recv_ref, table_ref, waves)
+    change[...] = change_of(range(domains // 2), count, (own_ref, mine_ref, beside_ref, recv_ref), table_ref, waves)
 
     def step(block, carry):
         at = column(block // per_pair)
@@ -527,22 +543,14 @@
     diag = diagonal.reshape(nblocks, LANES)
     offsets = xor_offsets(count)
 
-    def boundary(value):
-        edge = jnp.where(dom == 0, value[:, cells - LANES :], value[:, :LANES])
-        return xor_permute(edge, "dom", 1)
-
     block_rows = 2 * rows + 3 * SUB
     vmem = pl.BlockSpec(memory_space=pltpu.VMEM)
     smem = pl.BlockSpec(memory_space=pltpu.SMEM)
     ext_shape = (rows + 2 * SUB, cells + 2 * LANES)
-    across = boundary(field)
-    local, edge, strip, extended, field_in, sv_in, fw_in, nb_in, diag_in, iface_in = call(
-        functools.partial(source_kernel, planes),
+    lent, field_in, sv_in, fw_in, nb_in, diag_in, iface_in = call(
+        load_kernel,
         [
-            ((rows, cells), F32),
-            ((6, nblocks, LANES), F32),
-            ((SUB, cells), F32),
-            (ext_shape, F32),
+            ((rows, LANES), F32),
             ((rows, cells), F32),
             ((rows, cells), F32),
             (flux_weight.shape, F32),
@@ -550,9 +558,20 @@
             ((nblocks, LANES), F32),
             (interface.shape, jnp.int32),
         ],
-        (field, sv, flux_weight, neighbours, diag, interface),
+        (dom.reshape(1), field, sv, flux_weight, neighbours, diag, interface),
         [pltpu.SemaphoreType.DMA((6,))],
-        [HBM] * 6,
+        [smem] + [HBM] * 6,
+    )
+    across = xor_permute(lent, "dom", 1)
+    local, edge, strip, extended = call(
+        functools.partial(source_kernel, planes),
+        [
+            ((rows, cells), F32),
+            ((6, nblocks, LANES), F32),
+            ((SUB, cells), F32),
+            (ext_shape, F32),
+        ],
+        (field_in, sv_in, fw_in, nb_in, diag_in),
     )
     local, edge, strip, payload, dif = call(
         functools.partial(seam_kernel, planes),
@@ -568,7 +587,7 @@
         [smem] + [vmem] * 10,
         aliases={2: 0, 3: 1, 4: 2},
     )
-    mine, received = gathered(payload, "span")
+    blocks = gathered(payload, "span", apart=True)
 
     in_parts = lambda value: (value.shape[:2] + (2,) + value.shape[2:], BF16)
     slot_of, m1, m2, m3, root = call(
@@ -607,21 +626,21 @@
     s3, keep = call(
         functools.partial(up_kernel, offsets, rows),
         [((wave_rows, LANES), F32), ((waves, SUB, LANES), F32)],
-        (me.reshape(1), mine, received, table, edge_table, sigma, dif, m1, m2, m3),
+        (me.reshape(1), *blocks, table, edge_table, sigma, dif, m1, m2, m3),
         [
             pltpu.VMEM((count * rows, pair_cells), F32),
             pltpu.VMEM((count, 3 * SUB, 2 * LANES), F32),
             pltpu.VMEM((waves, SUB, LANES), F32),
             pltpu.VMEM((pair_cells // LANES, wave_rows, LANES), F32),
         ],
-        [smem] + [vmem] * 9,
+        [smem] + [vmem] * 11,
         limit=16,
     )
     other = xor_permute(s3, "dom", 1)
     (returned,) = call(
         down_kernel, [((pair_cells // LANES, wave_rows, LANES), F32)], (s3, other, keep, m1, m2, m3, root), limit=16
     )
-    mine, received = gathered(returned.reshape(-1, LANES), "span")
+    blocks = gathered(returned.reshape(-1, LANES), "span", apart=True)
 
     up_ring = [(i, (i + 1) % count) for i in range(count)]
     down_ring = [(j, i) for i, j in up_ring]
@@ -641,13 +660,13 @@
     flows = jnp.stack([left, right, at_first, at_last])
 
     wave_scratch = lambda pairs: pltpu.VMEM((count * wave_rows, pairs * LANES), F32)
-    parts = (mine, received, back_table, local, flows, diag_in, slot_of)
+    parts = (*blocks, back_table, local, flows, diag_in, slot_of)
     (rim,) = call(
         functools.partial(rim_kernel, planes, domains, count),
         [((rows, LANES), F32)],
         (dom.reshape(1),) + parts,
         [wave_scratch(1)],
-        [smem] + [vmem] * 7,
+        [smem] + [vmem] * 9,
     )
     halo = xor_permute(rim, "dom", 1)
     (extended,) = call(

time: 53.3 us -> 69.9 us (1.31)
  local copies, waits for them, and re-layouts: 0.59 us -> 8.18 us
  other arithmetic: 1.5 us -> 8.72 us
  waiting for transfers between devices: 18.1 us -> 15.7 us
  starting transfers between devices: 17.3 us -> 19.3 us
  Pallas kernels: 14.7 us -> 16.2 us
    unnamed x3 -> x88, local copies, waits for them, and re-layouts: 0.02 us -> 7.6 us
    ppermute x14 -> x16, starting transfers between devices: 11.6 us -> 13.7 us  [xor_permute(): lax.ppermute(value, axis, [(i, i ^ mask) for i in range(lax.axis_size(axi...]
    ppermute x14 -> x16, waiting for transfers between devices: 16.6 us -> 14.5 us  [xor_permute(): lax.ppermute(value, axis, [(i, i ^ mask) for i in range(lax.axis_size(axi...]
    another operation x4, other arithmetic: 0.04 us -> 1.99 us  [inflow(): other = xor_permute(jnp.stack([ahead, back]), 'span', size)]
    pallas_call x8 -> x9, Pallas kernels: 14.7 us -> 16.2 us  [call(): pl.pallas_call(kernel, out_shape=[jax.ShapeDtypeStruct(*out) for out in o...]
    select_n x2, other arithmetic: 0.05 us -> 1.13 us  [fourier_entry(): jnp.where(at_edge, math.sqrt(1.0 / PLANES), math.sqrt(2.0 / PLANES))]
    another operation x2, other arithmetic: 0.06 us -> 0.84 us  [on_device(): flows = jnp.stack([left, right, at_first, at_last])]
    select_n x1, other arithmetic: 0.04 us -> 0.78 us  [inflow(): jnp.where(is_right, ahead + squares[bit] * other[0], other[0] + squares[b...]
  transfers between devices with their start and end apart: 16 -> 18, of which waited for: 10 -> 10; matrix products, arithmetic and copies ran while one was open for 2% -> 13% of each run, Pallas kernels for 19% -> 18%
where the time goes in v2:
time: 69.9 us; the launch traced here: 69.2 us
  starting transfers between devices  19.3 us (28%)
  Pallas kernels  16.2 us (23%)
  waiting for transfers between devices  15.7 us (22%)
  other arithmetic  8.72 us (12%)
  local copies, waits for them, and re-layouts  8.18 us (12%)
  between operations  1.18 us (2%)
    pallas_call x9, Pallas kernels, call(): pl.pallas_call(kernel, out_shape=[jax.ShapeDtypeStruct(*out) for out in o...  16.2 us
    ppermute x16, waiting for transfers between devices, xor_permute(): lax.ppermute(value, axis, [(i, i ^ mask) for i in range(lax.axis_size(axi...  14.5 us
    ppermute x16, starting transfers between devices, xor_permute(): lax.ppermute(value, axis, [(i, i ^ mask) for i in range(lax.axis_size(axi...  13.7 us
    unnamed x88, local copies, waits for them, and re-layouts  7.6 us
    ppermute x1, starting transfers between devices, on_device(): lax.ppermute(v_first, 'span', down_ring)  3.04 us
    ppermute x1, starting transfers between devices, on_device(): lax.ppermute(v_last, 'span', up_ring)  2.52 us
    another operation x4, other arithmetic, inflow(): other = xor_permute(jnp.stack([ahead, back]), 'span', size)  1.99 us
  transfers between devices with their start and end apart: 18, of which 10 were waited for; matrix products, arithmetic and copies ran while one was open for 13% of the time, Pallas kernels for 18%

profile of v2, /device:TPU:0, one launch (start us, length us, event | category | flops | bytes accessed | tf_op | source)
XLA Modules:
  0.0 69.2 jit_solution(13583156801827462534)
XLA Ops:
  0.6 1.1 %shard_map.122 = (f32[16,128]{1,0:T(8,128)S(1)}, f32[16,4096]{1,0:T(8,128)S(1)}, f32[16,4096]{1,0:T(8,128)S(1)}, f32[4,4096]{1,0:T(4,128)S(1)}, s32[4,4096]{1,0:...) custom-call(s32[1]{0:T(128)} %bitcast.1.dom_ref, f32[16,4096]{1,0:T(8,128)} %v_hbm.1, f32[16,4096]{1,0:T(8,128)} %sv_hbm.1, ...), custom_call_target="tpu_custom_call" | custom-call | tf_op jit(solution)/shard_map/pallas_call | solution.py:481
  4.0 0.7 %select_multiply_fusion = f32[16,16]{1,0:T(8,128)} fusion(f32[16]{0:T(128)S(1)} %get-tuple-element.59, s32[16]{0:T(128)S(1)} %add.272, s32[16]{0:T(128)S(1)} %add_select_fusion.10, pred[16]{0:T(512)(128)(4,1)S(1)} %fusion.39), kind=kLoop, calls=%fused_computation.87 | loop fusion | flops 4096 | bytes 1232 | tf_op jit(solution)/shard_map/mul | solution.py:28
  4.7 0.7 %multiply_select_fusion.7.table_ref = f32[16,128]{1,0:T(8,128)} fusion(f32[16]{0:T(128)S(1)} %get-tuple-element.59, s32[128]{0:T(128)S(1)} %get-tuple-element.50, s32[16]{0:T(128)S(1)} %add_select_fusion.10, pred[16]{0:T(512)(128)(4,1)S(1)} %fusion.39, pred[128]{0:T(512)(128)(4,1)S(1)} %broadcast_in_dim.118), kind=kLoop, calls=%fused_computation.88 | loop fusion | flops 34816 | bytes 8976 | tf_op jit(solution)/shard_map/jit(_where)/select_n | solution.py:613
  6.1 1.7 %shard_map.123 = (f32[16,4096]{1,0:T(8,128)S(1)}, f32[6,32,128]{2,1,0:T(8,128)S(1)}, f32[8,4096]{1,0:T(8,128)S(1)}, f32[32,4352]{1,0:T(8,128)S(1)}) custom-call(f32[16,4096]{1,0:T(8,128)S(1)} %get-tuple-element.25.v_ref, f32[16,4096]{1,0:T(8,128)S(1)} %get-tuple-element.26.sv_ref, f32[4,4096]{1,0:T(4,128)S(1)} %get-tuple-element.27.fw_ref, ...), custom_call_target="tpu_custom_call" | custom-call | tf_op jit(solution)/shard_map/pallas_call | solution.py:481
  10.1 2.5 %collective-permute-start.12 = (f32[32,128]{1,0:T(8,128)S(1)}, f32[32,128]{1,0:T(8,128)S(1)}, u32[]{:S(2)}, u32[]{:S(2)}) collective-permute-start(f32[32,128]{1,0:T(8,128)S(1)} %get-tuple-element.54), channel_id=1, source_target_pairs={{0,2},{2,4},{4,6},{6,8},{8,10},{10,12},{12,14},{14,0},{1,3},{3,5},... | collective-permute-start | bytes 49160 | tf_op jit(solution)/shard_map/ppermute | solution.py:649
  12.6 3.0 %collective-permute-start.13 = (f32[32,128]{1,0:T(8,128)S(1)}, f32[32,128]{1,0:T(8,128)S(1)}, u32[]{:S(2)}, u32[]{:S(2)}) collective-permute-start(f32[32,128]{1,0:T(8,128)S(1)} %get-tuple-element.53), channel_id=1, source_target_pairs={{2,0},{4,2},{6,4},{8,6},{10,8},{12,10},{14,12},{0,14},{3,1},{5,3},... | collective-permute-start | bytes 49160 | tf_op jit(solution)/shard_map/ppermute | solution.py:649
  16.2 1.2 %collective-permute-done.12 = f32[32,128]{1,0:T(8,128)S(1)} collective-permute-done((f32[32,128]{1,0:T(8,128)S(1)}, f32[32,128]{1,0:T(8,128)S(1)}, u32[]{:S(2)}, u32[]{:S(2)}) %collective-permute-start.12) | collective-permute-done | bytes 16416 | tf_op jit(solution)/shard_map/ppermute | solution.py:649
  18.1 1.4 %collective-permute-start.14 = (f32[2,32,128]{2,1,0:T(8,128)}, f32[2,32,128]{2,1,0:T(8,128)}, u32[]{:S(2)}, u32[]{:S(2)}) collective-permute-start(f32[2,32,128]{2,1,0:T(8,128)} %pad_maximum_fusion.1), channel_id=1, source_target_pairs={{0,2},{2,0},{4,6},{6,4},{8,10},{10,8},{12,14},{14,12},{1,3},{3,1},... | collective-permute-start | bytes 98312 | tf_op jit(solution)/shard_map/ppermute | solution.py:38
  20.8 3.6 %shard_map.125 = (s32[32,128]{1,0:T(8,128)S(1)}, bf16[16,4,2,128,128]{4,3,2,1,0:T(8,128)(2,1)S(1)}, bf16[16,2,2,128,128]{4,3,2,1,0:T(8,128)(2,1)S(1)}, bf16[16,1...) custom-call(s32[8,128]{1,0:T(8,128)S(1)} %copy-done.17, f32[16,4,128,128]{3,2,1,0:T(8,128)} %m1_hbm.1, ...), custom_call_target="tpu_custom_call" | custom-call | tf_op jit(solution)/shard_map/pallas_call | solution.py:481
  24.4 1.6 %collective-permute-start.1 = (f32[56,256]{1,0:T(8,128)S(1)}, f32[56,256]{1,0:T(8,128)S(1)}, u32[]{:S(2)}, u32[]{:S(2)}) collective-permute-start(f32[56,256]{1,0:T(8,128)S(1)} %copy-done.14), channel_id=1, source_target_pairs={{0,4},{2,6},{4,0},{6,2},{8,12},{10,14},{12,8},{14,10},{1,5},{3,7},... | collective-permute-start | bytes 172040 | tf_op jit(solution)/shard_map/ppermute | solution.py:38
  26.1 2.9 %collective-permute-start.2 = (f32[56,256]{1,0:T(8,128)S(1)}, f32[56,256]{1,0:T(8,128)S(1)}, u32[]{:S(2)}, u32[]{:S(2)}) collective-permute-start(f32[56,256]{1,0:T(8,128)S(1)} %copy-done.14), channel_id=1, source_target_pairs={{0,8},{2,10},{4,12},{6,14},{8,0},{10,2},{12,4},{14,6},{1,9},{3,11}... | collective-permute-start | bytes 172040 | tf_op jit(solution)/shard_map/ppermute | solution.py:38
  29.5 0.8 %fusion.30 = (f32[1,32,128]{2,1,0:T(8,128)S(1)}, f32[1,32,128]{2,1,0:T(8,128)S(1)}) fusion(f32[32,128]{1,0:T(8,128)S(1)} %copy-done.21, f32[2,32,128]{2,1,0:T(8,128)} %collective-permute-done.14, pred[]{:T(512)S(6)} %eq.102, f32[32,128]{1,0:T(8,128)S(1)} %get-tuple-element.29.diag_ref, f32[32,128]{1,0:T(8,128)S(1)} %copy-done.23), kind=kLoop, calls=%fused_computation.90 | loop fusion | flops 86016 | bytes 114689 | tf_op jit(solution)/shard_map/stack | solution.py:514
  30.5 1.4 %collective-permute-done.2 = f32[56,256]{1,0:T(8,128)S(1)} collective-permute-done((f32[56,256]{1,0:T(8,128)S(1)}, f32[56,256]{1,0:T(8,128)S(1)}, u32[]{:S(2)}, u32[]{:S(2)}) %collective-permute-start.2) | collective-permute-done | bytes 57376 | tf_op jit(solution)/shard_map/ppermute | solution.py:38
  31.9 3.0 %collective-permute-done.3 = f32[56,256]{1,0:T(8,128)S(1)} collective-permute-done((f32[56,256]{1,0:T(8,128)S(1)}, f32[56,256]{1,0:T(8,128)S(1)}, u32[]{:S(2)}, u32[]{:S(2)}) %collective-permute-start.3) | collective-permute-done | bytes 57376 | tf_op jit(solution)/shard_map/ppermute | solution.py:38
  35.4 0.8 %fusion.13 = (f32[32,128]{1,0:T(8,128)S(1)}, f32[32,128]{1,0:T(8,128)S(1)}) fusion(f32[2,32,128]{2,1,0:T(8,128)S(1)} %collective-permute-done.15, pred[]{:T(512)S(6)} %eq.101, f32[32,128]{1,0:T(8,128)S(1)} %copy-done.21, f32[2,32,128]{2,1,0:T(8,128)} %collective-permute-done.14, pred[]{:T(512)S(6)} %eq.102, f32[32,128]{1,0:T(8,128)S(1)} %get-tuple-element.29.diag_ref, ...), kind=kLoop, calls=%fused_computation.47 | loop fusion | flops 131072 | bytes 147458 | tf_op jit(solution)/shard_map/jit(_where)/select_n | solution.py:521
  36.8 1.0 %collective-permute-start.16 = (f32[2,32,128]{2,1,0:T(8,128)}, f32[2,32,128]{2,1,0:T(8,128)}, u32[]{:S(2)}, u32[]{:S(2)}) collective-permute-start(f32[2,32,128]{2,1,0:T(8,128)} %pad_maximum_fusion.3), channel_id=1, source_target_pairs={{0,8},{2,10},{4,12},{6,14},{8,0},{10,2},{12,4},{14,6},{1,9},{3,11}... | collective-permute-start | bytes 98312 | tf_op jit(solution)/shard_map/ppermute | solution.py:38
  37.8 2.6 %collective-permute-done.5.recv_ref = f32[168,256]{1,0:T(8,128)S(1)} collective-permute-done((f32[168,256]{1,0:T(8,128)S(1)}, f32[168,256]{1,0:T(8,128)S(1)}, u32[]{:S(2)}, u32[]{:S(2)}) %collective-permute-start.5) | collective-permute-done | bytes 172064 | tf_op jit(solution)/shard_map/ppermute | solution.py:38
  40.6 3.1 %shard_map.126 = (f32[16,128]{1,0:T(8,128)}, f32[16,8,128]{2,1,0:T(8,128)S(1)}) custom-call(s32[1]{0:T(128)} %bitcast.me_ref, f32[56,256]{1,0:T(8,128)S(1)} %copy-done.14, f32[168,256]{1,0:T(8,128)S(1)} %constant_dynamic-update-slice_fusion.mine_ref, f32[56,256]{1,0:T(8,128)S(1)} %collective-permute-done.4.beside_ref, ...), custom_call_target="tpu_custom_call" | custom-call | tf_op jit(solution)/shard_map/pallas_call | solution.py:481
  44.5 0.7 %multiply_select_fusion.6.table_ref = f32[24,128]{1,0:T(8,128)} fusion(f32[128]{0:T(128)S(1)} %copy-done.40, s32[24]{0:T(128)S(1)} %copy-done.41, s32[128]{0:T(128)S(1)} %copy-done.39, pred[128]{0:T(512)(128)(4,1)S(1)} %copy-done.35, pred[128]{0:T(512)(128)(4,1)S(1)} %copy-done.37), kind=kLoop, calls=%fused_computation.76 | loop fusion | flops 52224 | bytes 13664 | tf_op jit(solution)/shard_map/jit(_where)/select_n | solution.py:624
  45.2 0.7 %collective-permute-done.6.other_ref = f32[16,128]{1,0:T(8,128)} collective-permute-done((f32[16,128]{1,0:T(8,128)}, f32[16,128]{1,0:T(8,128)}, u32[]{:S(2)}, u32[]{:S(2)}) %collective-permute-start.6) | collective-permute-done | bytes 8224 | tf_op jit(solution)/shard_map/ppermute | solution.py:38
  45.9 2.2 %copy-done.1 = bf16[16,4,2,128,128]{4,3,2,1,0:T(8,128)(2,1)S(1)} copy-done((bf16[16,4,2,128,128]{4,3,2,1,0:T(8,128)(2,1)S(1)}, bf16[16,4,2,128,128]{4,3,2,1,0:T(8,128)(2,1)}, u32[]{:S(2)}) %copy-start.1) | copy-done | bytes 4194328
  48.1 1.2 %copy-done.7 = bf16[16,1,2,128,128]{4,3,2,1,0:T(8,128)(2,1)S(1)} copy-done((bf16[16,1,2,128,128]{4,3,2,1,0:T(8,128)(2,1)S(1)}, bf16[16,1,2,128,128]{4,3,2,1,0:T(8,128)(2,1)}, u32[]{:S(2)}) %copy-start.7) | copy-done | bytes 1048600
  49.3 0.8 %copy-done.10 = f32[16,8,128]{2,1,0:T(8,128)S(1)} copy-done((f32[16,8,128]{2,1,0:T(8,128)S(1)}, f32[16,8,128]{2,1,0:T(8,128)}, u32[]{:S(2)}) %copy-start.10) | copy-done | bytes 65560
  50.2 2.7 %shard_map.127 = f32[4,16,128]{2,1,0:T(8,128)S(1)} custom-call(f32[16,128]{1,0:T(8,128)} %get-tuple-element.40.s3_ref, f32[16,128]{1,0:T(8,128)} %collective-permute-done.6.other_ref, f32[16,8,128]{2,1,0:T(8,128)S(1)} %copy-done.10, bf16[16,4,2,128,128]{4,3,2,1,0:T(8,128)(2,1)S(1)} %copy-done.1, bf16[16,2,2,128,128]{4,3,2,1,0:T(8,128)(2,1)S(1)} %get-tuple-element.38.m2, ...), custom_call_target="tpu_custom_call" | custom-call | tf_op jit(solution)/shard_map/pallas_call | solution.py:481
  53.0 0.8 %fusion.4 = (f32[1,32,128]{2,1,0:T(8,128)S(1)}, f32[1,32,128]{2,1,0:T(8,128)S(1)}) fusion(f32[32,128]{1,0:T(8,128)S(1)} %copy-done.25, f32[2,32,128]{2,1,0:T(8,128)} %collective-permute-done.16, f32[2,32,128]{2,1,0:T(8,128)} %collective-permute-done.14, f32[2,32,128]{2,1,0:T(8,128)S(1)} %copy-done.33, pred[]{:T(512)S(6)} %eq.105, pred[]{:T(512)S(6)} %eq.104, ...), kind=kLoop, calls=%fused_computation.20 | loop fusion | flops 245760 | bytes 180233 | tf_op jit(solution)/shard_map/stack | solution.py:660
  53.8 1.3 %collective-permute-start.8 = (f32[64,128]{1,0:T(8,128)S(1)}, f32[64,128]{1,0:T(8,128)S(1)}, u32[]{:S(2)}, u32[]{:S(2)}) collective-permute-start(f32[64,128]{1,0:T(8,128)S(1)} %bitcast.83), channel_id=1, source_target_pairs={{0,8},{2,10},{4,12},{6,14},{8,0},{10,2},{12,4},{14,6},{1,9},{3,11}... | collective-permute-start | bytes 98312 | tf_op jit(solution)/shard_map/ppermute | solution.py:38
  55.1 3.1 %collective-permute-start.9 = (f32[64,128]{1,0:T(8,128)S(1)}, f32[64,128]{1,0:T(8,128)S(1)}, u32[]{:S(2)}, u32[]{:S(2)}) collective-permute-start(f32[64,128]{1,0:T(8,128)S(1)} %bitcast.84), channel_id=1, source_target_pairs={{0,12},{2,14},{4,8},{6,10},{8,4},{10,6},{12,0},{14,2},{1,13},{3,15... | collective-permute-start | bytes 98312 | tf_op jit(solution)/shard_map/ppermute | solution.py:38
  58.7 2.1 %collective-permute-done.9 = f32[64,128]{1,0:T(8,128)S(1)} collective-permute-done((f32[64,128]{1,0:T(8,128)S(1)}, f32[64,128]{1,0:T(8,128)S(1)}, u32[]{:S(2)}, u32[]{:S(2)}) %collective-permute-start.9) | collective-permute-done | bytes 32800 | tf_op jit(solution)/shard_map/ppermute | solution.py:38
  61.1 1.3 %collective-permute-done.10.beside_ref = f32[64,128]{1,0:T(8,128)S(1)} collective-permute-done((f32[64,128]{1,0:T(8,128)S(1)}, f32[64,128]{1,0:T(8,128)S(1)}, u32[]{:S(2)}, u32[]{:S(2)}) %collective-permute-start.10) | collective-permute-done | bytes 32800 | tf_op jit(solution)/shard_map/ppermute | solution.py:38
  62.4 3.1 %collective-permute-done.11.recv_ref = f32[192,128]{1,0:T(8,128)S(1)} collective-permute-done((f32[192,128]{1,0:T(8,128)S(1)}, f32[192,128]{1,0:T(8,128)S(1)}, u32[]{:S(2)}, u32[]{:S(2)}) %collective-permute-start.11) | collective-permute-done | bytes 98336 | tf_op jit(solution)/shard_map/ppermute | solution.py:38
  65.8 1.1 %shard_map.128.ext_in = f32[32,4352]{1,0:T(8,128)S(1)} custom-call(f32[64,128]{1,0:T(8,128)S(1)} %bitcast.87, f32[192,128]{1,0:T(8,128)S(1)} %constant_dynamic-update-slice_fusion.3.mine_ref, f32[64,128]{1,0:T(8,128)S(1)} %collective-permute-done.10.beside_ref, f32[192,128]{1,0:T(8,128)S(1)} %collective-permute-done.11.recv_ref, f32[24,128]{1,0:T(8,128)S(1)} %copy-done.8, ...), custom_call_target="tpu_custom_call" | custom-call | tf_op jit(solution)/shard_map/pallas_call | solution.py:481
  66.9 2.3 %shard_map.130 = (f32[16,4096]{1,0:T(8,128)}, f32[16,4096]{1,0:T(8,128)}) custom-call(f32[32,4352]{1,0:T(8,128)S(1)} %shard_map.128.ext_in, f32[16,4096]{1,0:T(8,128)S(1)} %copy-done.5, f32[16,128]{1,0:T(8,128)S(1)} %collective-permute-done.17.halo_ref, f32[16,4096]{1,0:T(8,128)S(1)} %get-tuple-element.26.sv_ref, f32[4,4096]{1,0:T(4,128)S(1)} %get-tuple-element.27.fw_ref, ...), custom_call_target="tpu_custom_call" | custom-call | tf_op jit(solution)/shard_map/pallas_call | solution.py:481
  (137 shorter events, 11.3 us)
Async XLA Ops:
  1.7 18.3 %copy-start.4 = (f32[16,4096]{1,0:T(8,128)}, f32[16,4096]{1,0:T(8,128)S(1)}, u32[]{:S(2)}) copy-start(f32[16,4096]{1,0:T(8,128)S(1)} %get-tuple-element.25.v_ref) | copy-start | bytes 786436
  1.7 18.3 %copy-start.16 = (s32[8,128]{1,0:T(8,128)}, s32[8,128]{1,0:T(8,128)S(1)}, u32[]{:S(2)}) copy-start(s32[8,128]{1,0:T(8,128)S(1)} %get-tuple-element.34.iface_ref) | copy-start | bytes 12292
  1.8 6.0 %collective-permute-start = (f32[16,128]{1,0:T(8,128)S(1)}, f32[16,128]{1,0:T(8,128)S(1)}, u32[]{:S(2)}, u32[]{:S(2)}) collective-permute-start(f32[16,128]{1,0:T(8,128)S(1)} %get-tuple-element.24), channel_id=1, source_target_pairs={{0,1},{1,0},{2,3},{3,2},{4,5},{5,4},{6,7},{7,6},{8,9},{9,8},{10,11... | collective-permute-start | bytes 24584 | tf_op jit(solution)/shard_map/ppermute | solution.py:38
  10.1 7.3 %collective-permute-start.12 = (f32[32,128]{1,0:T(8,128)S(1)}, f32[32,128]{1,0:T(8,128)S(1)}, u32[]{:S(2)}, u32[]{:S(2)}) collective-permute-start(f32[32,128]{1,0:T(8,128)S(1)} %get-tuple-element.54), channel_id=1, source_target_pairs={{0,2},{2,4},{4,6},{6,8},{8,10},{10,12},{12,14},{14,0},{1,3},{3,5},... | collective-permute-start | bytes 49160 | tf_op jit(solution)/shard_map/ppermute | solution.py:649
  12.6 4.8 %collective-permute-start.13 = (f32[32,128]{1,0:T(8,128)S(1)}, f32[32,128]{1,0:T(8,128)S(1)}, u32[]{:S(2)}, u32[]{:S(2)}) collective-permute-start(f32[32,128]{1,0:T(8,128)S(1)} %get-tuple-element.53), channel_id=1, source_target_pairs={{2,0},{4,2},{6,4},{8,6},{10,8},{12,10},{14,12},{0,14},{3,1},{5,3},... | collective-permute-start | bytes 49160 | tf_op jit(solution)/shard_map/ppermute | solution.py:649
  18.1 11.5 %collective-permute-start.14 = (f32[2,32,128]{2,1,0:T(8,128)}, f32[2,32,128]{2,1,0:T(8,128)}, u32[]{:S(2)}, u32[]{:S(2)}) collective-permute-start(f32[2,32,128]{2,1,0:T(8,128)} %pad_maximum_fusion.1), channel_id=1, source_target_pairs={{0,2},{2,0},{4,6},{6,4},{8,10},{10,8},{12,14},{14,12},{1,3},{3,1},... | collective-permute-start | bytes 98312 | tf_op jit(solution)/shard_map/ppermute | solution.py:38
  20.7 19.7 %copy-start.34 = (f32[16,16]{1,0:T(8,128)S(1)}, f32[16,16]{1,0:T(8,128)}, u32[]{:S(2)}) copy-start(f32[16,16]{1,0:T(8,128)} %select_multiply_fusion) | copy-start | bytes 3076
  20.7 19.8 %copy-start.38 = (f32[16]{0:T(128)S(1)}, f32[16]{0:T(128)}, u32[]{:S(2)}) copy-start(f32[16]{0:T(128)} %get-tuple-element.60) | copy-start | bytes 196
  20.7 19.9 %copy-start.15 = (f32[16,128]{1,0:T(8,128)S(1)}, f32[16,128]{1,0:T(8,128)}, u32[]{:S(2)}) copy-start(f32[16,128]{1,0:T(8,128)} %multiply_select_fusion.7.table_ref) | copy-start | bytes 24580
  20.8 19.9 %copy-start.19 = (f32[8,128]{1,0:T(8,128)S(1)}, f32[8,128]{1,0:T(8,128)}, u32[]{:S(2)}) copy-start(f32[8,128]{1,0:T(8,128)} %copy-done.18) | copy-start | bytes 12292
  24.4 19.4 %copy-start = (bf16[16,4,2,128,128]{4,3,2,1,0:T(8,128)(2,1)}, bf16[16,4,2,128,128]{4,3,2,1,0:T(8,128)(2,1)S(1)}, u32[]{:S(2)}) copy-start(bf16[16,4,2,128,128]{4,3,2,1,0:T(8,128)(2,1)S(1)} %get-tuple-element.37.m1) | copy-start | bytes 12582916
  24.4 19.4 %copy-start.6 = (bf16[16,1,2,128,128]{4,3,2,1,0:T(8,128)(2,1)}, bf16[16,1,2,128,128]{4,3,2,1,0:T(8,128)(2,1)S(1)}, u32[]{:S(2)}) copy-start(bf16[16,1,2,128,128]{4,3,2,1,0:T(8,128)(2,1)S(1)} %get-tuple-element.42.root) | copy-start | bytes 3145732
  24.4 19.4 %copy-start.11 = (s32[32,128]{1,0:T(8,128)}, s32[32,128]{1,0:T(8,128)S(1)}, u32[]{:S(2)}) copy-start(s32[32,128]{1,0:T(8,128)S(1)} %get-tuple-element.45.inv_ref) | copy-start | bytes 49156
  24.4 6.0 %collective-permute-start.1 = (f32[56,256]{1,0:T(8,128)S(1)}, f32[56,256]{1,0:T(8,128)S(1)}, u32[]{:S(2)}, u32[]{:S(2)}) collective-permute-start(f32[56,256]{1,0:T(8,128)S(1)} %copy-done.14), channel_id=1, source_target_pairs={{0,4},{2,6},{4,0},{6,2},{8,12},{10,14},{12,8},{14,10},{1,5},{3,7},... | collective-permute-start | bytes 172040 | tf_op jit(solution)/shard_map/ppermute | solution.py:38
  26.1 5.8 %collective-permute-start.2 = (f32[56,256]{1,0:T(8,128)S(1)}, f32[56,256]{1,0:T(8,128)S(1)}, u32[]{:S(2)}, u32[]{:S(2)}) collective-permute-start(f32[56,256]{1,0:T(8,128)S(1)} %copy-done.14), channel_id=1, source_target_pairs={{0,8},{2,10},{4,12},{6,14},{8,0},{10,2},{12,4},{14,6},{1,9},{3,11}... | collective-permute-start | bytes 172040 | tf_op jit(solution)/shard_map/ppermute | solution.py:38
  29.0 6.0 %collective-permute-start.3 = (f32[56,256]{1,0:T(8,128)S(1)}, f32[56,256]{1,0:T(8,128)S(1)}, u32[]{:S(2)}, u32[]{:S(2)}) collective-permute-start(f32[56,256]{1,0:T(8,128)S(1)} %copy-done.14), channel_id=1, source_target_pairs={{0,12},{2,14},{4,8},{6,10},{8,4},{10,6},{12,0},{14,2},{1,13},{3,15... | collective-permute-start | bytes 172040 | tf_op jit(solution)/shard_map/ppermute | solution.py:38
  29.0 8.9 %collective-permute-start.4 = (f32[56,256]{1,0:T(8,128)S(1)}, f32[56,256]{1,0:T(8,128)S(1)}, u32[]{:S(2)}, u32[]{:S(2)}) collective-permute-start(f32[56,256]{1,0:T(8,128)S(1)} %copy-done.14), channel_id=1, source_target_pairs={{0,2},{2,0},{4,6},{6,4},{8,10},{10,8},{12,14},{14,12},{1,3},{3,1},... | collective-permute-start | bytes 172040 | tf_op jit(solution)/shard_map/ppermute | solution.py:38
  30.3 5.1 %collective-permute-start.15 = (f32[2,32,128]{2,1,0:T(8,128)S(1)}, f32[2,32,128]{2,1,0:T(8,128)S(1)}, u32[]{:S(2)}, u32[]{:S(2)}) collective-permute-start(f32[2,32,128]{2,1,0:T(8,128)S(1)} %pad_maximum_fusion.2), channel_id=1, source_target_pairs={{0,4},{2,6},{4,0},{6,2},{8,12},{10,14},{12,8},{14,10},{1,5},{3,7},... | collective-permute-start | bytes 98312 | tf_op jit(solution)/shard_map/ppermute | solution.py:38
  35.0 5.5 %collective-permute-start.5 = (f32[168,256]{1,0:T(8,128)S(1)}, f32[168,256]{1,0:T(8,128)S(1)}, u32[]{:S(2)}, u32[]{:S(2)}) collective-permute-start(f32[168,256]{1,0:T(8,128)S(1)} %constant_dynamic-update-slice_fusion.mine_ref), channel_id=1, source_target_pairs={{0,2},{2,0},{4,6},{6,4},{8,10},{10,8},{12,14},{14,12},{1,3},{3,1},... | collective-permute-start | bytes 516104 | tf_op jit(solution)/shard_map/ppermute | solution.py:38
  36.8 16.1 %collective-permute-start.16 = (f32[2,32,128]{2,1,0:T(8,128)}, f32[2,32,128]{2,1,0:T(8,128)}, u32[]{:S(2)}, u32[]{:S(2)}) collective-permute-start(f32[2,32,128]{2,1,0:T(8,128)} %pad_maximum_fusion.3), channel_id=1, source_target_pairs={{0,8},{2,10},{4,12},{6,14},{8,0},{10,2},{12,4},{14,6},{1,9},{3,11}... | collective-permute-start | bytes 98312 | tf_op jit(solution)/shard_map/ppermute | solution.py:38
  44.4 1.5 %collective-permute-start.6 = (f32[16,128]{1,0:T(8,128)}, f32[16,128]{1,0:T(8,128)}, u32[]{:S(2)}, u32[]{:S(2)}) collective-permute-start(f32[16,128]{1,0:T(8,128)} %get-tuple-element.40.s3_ref), channel_id=1, source_target_pairs={{0,1},{1,0},{2,3},{3,2},{4,5},{5,4},{6,7},{7,6},{8,9},{9,8},{10,11... | collective-permute-start | bytes 24584 | tf_op jit(solution)/shard_map/ppermute | solution.py:38
  50.2 10.9 %copy-start.29 = (f32[32,128]{1,0:T(8,128)S(1)}, f32[32,128]{1,0:T(8,128)}, u32[]{:S(2)}) copy-start(f32[32,128]{1,0:T(8,128)} %copy-done.28) | copy-start | bytes 49156
  50.2 15.3 %copy-start.3 = (f32[16,4096]{1,0:T(8,128)S(1)}, f32[16,4096]{1,0:T(8,128)}, u32[]{:S(2)}) copy-start(f32[16,4096]{1,0:T(8,128)} %copy-done.2) | copy-start | bytes 786436
  50.2 15.3 %copy-start.8 = (f32[24,128]{1,0:T(8,128)S(1)}, f32[24,128]{1,0:T(8,128)}, u32[]{:S(2)}) copy-start(f32[24,128]{1,0:T(8,128)} %multiply_select_fusion.6.table_ref) | copy-start | bytes 36868
  50.2 15.3 %copy-start.12 = (s32[32,128]{1,0:T(8,128)S(1)}, s32[32,128]{1,0:T(8,128)}, u32[]{:S(2)}) copy-start(s32[32,128]{1,0:T(8,128)} %copy-done.11) | copy-start | bytes 49156
  50.2 16.7 %copy-start.5 = (f32[16,4096]{1,0:T(8,128)S(1)}, f32[16,4096]{1,0:T(8,128)}, u32[]{:S(2)}) copy-start(f32[16,4096]{1,0:T(8,128)} %copy-done.4) | copy-start | bytes 786436
  52.9 5.7 %collective-permute-start.7 = (f32[64,128]{1,0:T(8,128)S(1)}, f32[64,128]{1,0:T(8,128)S(1)}, u32[]{:S(2)}, u32[]{:S(2)}) collective-permute-start(f32[64,128]{1,0:T(8,128)S(1)} %bitcast.82), channel_id=1, source_target_pairs={{0,4},{2,6},{4,0},{6,2},{8,12},{10,14},{12,8},{14,10},{1,5},{3,7},... | collective-permute-start | bytes 98312 | tf_op jit(solution)/shard_map/ppermute | solution.py:38
  53.8 4.9 %collective-permute-start.8 = (f32[64,128]{1,0:T(8,128)S(1)}, f32[64,128]{1,0:T(8,128)S(1)}, u32[]{:S(2)}, u32[]{:S(2)}) collective-permute-start(f32[64,128]{1,0:T(8,128)S(1)} %bitcast.83), channel_id=1, source_target_pairs={{0,8},{2,10},{4,12},{6,14},{8,0},{10,2},{12,4},{14,6},{1,9},{3,11}... | collective-permute-start | bytes 98312 | tf_op jit(solution)/shard_map/ppermute | solution.py:38
  55.1 5.7 %collective-permute-start.9 = (f32[64,128]{1,0:T(8,128)S(1)}, f32[64,128]{1,0:T(8,128)S(1)}, u32[]{:S(2)}, u32[]{:S(2)}) collective-permute-start(f32[64,128]{1,0:T(8,128)S(1)} %bitcast.84), channel_id=1, source_target_pairs={{0,12},{2,14},{4,8},{6,10},{8,4},{10,6},{12,0},{14,2},{1,13},{3,15... | collective-permute-start | bytes 98312 | tf_op jit(solution)/shard_map/ppermute | solution.py:38
  58.3 4.2 %collective-permute-start.10 = (f32[64,128]{1,0:T(8,128)S(1)}, f32[64,128]{1,0:T(8,128)S(1)}, u32[]{:S(2)}, u32[]{:S(2)}) collective-permute-start(f32[64,128]{1,0:T(8,128)S(1)} %bitcast.85), channel_id=1, source_target_pairs={{0,2},{2,0},{4,6},{6,4},{8,10},{10,8},{12,14},{14,12},{1,3},{3,1},... | collective-permute-start | bytes 98312 | tf_op jit(solution)/shard_map/ppermute | solution.py:38
  60.9 4.6 %collective-permute-start.11 = (f32[192,128]{1,0:T(8,128)S(1)}, f32[192,128]{1,0:T(8,128)S(1)}, u32[]{:S(2)}, u32[]{:S(2)}) collective-permute-start(f32[192,128]{1,0:T(8,128)S(1)} %constant_dynamic-update-slice_fusion.3.mine_ref), channel_id=1, source_target_pairs={{0,2},{2,0},{4,6},{6,4},{8,10},{10,8},{12,14},{14,12},{1,3},{3,1},... | collective-permute-start | bytes 294920 | tf_op jit(solution)/shard_map/ppermute | solution.py:38
  65.7 1.2 %collective-permute-start.17 = (f32[16,128]{1,0:T(8,128)S(1)}, f32[16,128]{1,0:T(8,128)S(1)}, u32[]{:S(2)}, u32[]{:S(2)}) collective-permute-start(f32[16,128]{1,0:T(8,128)S(1)} %shard_map.129), channel_id=1, source_target_pairs={{0,1},{1,0},{2,3},{3,2},{4,5},{5,4},{6,7},{7,6},{8,9},{9,8},{10,11... | collective-permute-start | bytes 24584 | tf_op jit(solution)/shard_map/ppermute | solution.py:38
  (28 other events, 134.1 us)

commit v3 on v2

--- a/solution.py
+++ b/solution.py
@@ -40,7 +40,9 @@
 
 def gathered(block, axis, apart=False):
     count = lax.axis_size(axis)
-    far = [xor_permute(block, axis, mask) for mask in range(count - 2, 0, -2)][::-1]
+    far = []
+    for mask in range(2, count, 2):
+        far.append(xor_permute(block, axis, mask))
     if not apart:
         mine = jnp.concatenate([block] + far, axis=0)
         return mine, xor_permute(mine, axis, 1)
@@ -170,10 +172,13 @@
 
 def seam_kernel(
     planes, dom_ref, halo_ref, q_in, edge_in, strip_in, ext, sv_ref, fw_ref, nb_ref, diag_ref, iface_ref,
-    q_ref, edge_ref, strip, pay_ref, dif_ref, window,
+    q_ref, edge_ref, pay_ref, dif_ref, window, strip,
 ):
     rows, cells = q_ref.shape
     nblocks = cells // LANES
+    q_ref[...] = q_in[...]
+    edge_ref[...] = edge_in[...]
+    strip[...] = strip_in[...]
     for side, block in ((0, nblocks - 1), (1, 0)):
 
         @pl.when(dom_ref[0] == side)
@@ -477,7 +482,7 @@
 MEBI = 1024 * 1024
 
 
-def call(kernel, outs, args, scratch=(), specs=None, out_specs=None, aliases=None, limit=8):
+def call(kernel, outs, args, scratch=(), specs=None, out_specs=None, limit=8):
     return pl.pallas_call(
         kernel,
         out_shape=[jax.ShapeDtypeStruct(*out) for out in outs],
@@ -485,7 +490,6 @@
         out_specs=out_specs or whole(*outs),
         scratch_shapes=list(scratch),
         compiler_params=pltpu.CompilerParams(vmem_limit_bytes=limit * MEBI),
-        input_output_aliases=aliases or {},
     )(*(in_hbm(arg) if spec is HBM else arg for arg, spec in zip(args, specs or whole(*args))))
 
 
@@ -573,19 +577,17 @@
         ],
         (field_in, sv_in, fw_in, nb_in, diag_in),
     )
-    local, edge, strip, payload, dif = call(
+    local, edge, payload, dif = call(
         functools.partial(seam_kernel, planes),
         [
             ((rows, cells), F32),
             ((6, nblocks, LANES), F32),
-            ((SUB, cells), F32),
             ((block_rows, 2 * LANES), F32),
             ((domains, LANES), F32),
         ],
         (dom.reshape(1), across, local, edge, strip, extended, sv_in, fw_in, nb_in, diag_in, iface_in),
-        [pltpu.VMEM((rows + 2 * SUB, 3 * LANES), F32)],
+        [pltpu.VMEM((rows + 2 * SUB, 3 * LANES), F32), pltpu.VMEM((SUB, cells), F32)],
         [smem] + [vmem] * 10,
-        aliases={2: 0, 3: 1, 4: 2},
     )
     blocks = gathered(payload, "span", apart=True)
 

time: 69.9 us -> 69.9 us (level)
  transfers between devices with their start and end apart: 18 -> 18, of which waited for: 10 -> 10; matrix products, arithmetic and copies ran while one was open for 13% -> 12% of each run, Pallas kernels for 18% -> 18%
where the time goes in v3:
time: 69.9 us; the launch traced here: 69.3 us
  starting transfers between devices  19.3 us (28%)
  Pallas kernels  16.2 us (23%)
  waiting for transfers between devices  15.7 us (22%)
  other arithmetic  8.72 us (12%)
  local copies, waits for them, and re-layouts  8.18 us (12%)
  between operations  1.19 us (2%)
    pallas_call x9, Pallas kernels, call(): pl.pallas_call(kernel, out_shape=[jax.ShapeDtypeStruct(*out) for out in o...  16.2 us
    ppermute x16, waiting for transfers between devices, xor_permute(): lax.ppermute(value, axis, [(i, i ^ mask) for i in range(lax.axis_size(axi...  14.5 us
    ppermute x16, starting transfers between devices, xor_permute(): lax.ppermute(value, axis, [(i, i ^ mask) for i in range(lax.axis_size(axi...  13.7 us
    unnamed x88, local copies, waits for them, and re-layouts  7.6 us
    ppermute x1, starting transfers between devices, on_device(): lax.ppermute(v_first, 'span', down_ring)  3.04 us
    ppermute x1, starting transfers between devices, on_device(): lax.ppermute(v_last, 'span', up_ring)  2.52 us
    another operation x4, other arithmetic, inflow(): other = xor_permute(jnp.stack([ahead, back]), 'span', size)  1.99 us
  transfers between devices with their start and end apart: 18, of which 10 were waited for; matrix products, arithmetic and copies ran while one was open for 12% of the time, Pallas kernels for 18%

profile of v3, /device:TPU:0, one launch (start us, length us, event | category | flops | bytes accessed | tf_op | source)
XLA Modules:
  0.0 69.3 jit_solution(558186309101621270)
XLA Ops:
  0.6 1.1 %shard_map.122 = (f32[16,128]{1,0:T(8,128)S(1)}, f32[16,4096]{1,0:T(8,128)S(1)}, f32[16,4096]{1,0:T(8,128)S(1)}, f32[4,4096]{1,0:T(4,128)S(1)}, s32[4,4096]{1,0:...) custom-call(s32[1]{0:T(128)} %bitcast.1.dom_ref, f32[16,4096]{1,0:T(8,128)} %v_hbm.1, f32[16,4096]{1,0:T(8,128)} %sv_hbm.1, ...), custom_call_target="tpu_custom_call" | custom-call | tf_op jit(solution)/shard_map/pallas_call | solution.py:486
  4.0 0.7 %select_multiply_fusion = f32[16,16]{1,0:T(8,128)} fusion(f32[16]{0:T(128)S(1)} %get-tuple-element.59, s32[16]{0:T(128)S(1)} %add.272, s32[16]{0:T(128)S(1)} %add_select_fusion.10, pred[16]{0:T(512)(128)(4,1)S(1)} %fusion.39), kind=kLoop, calls=%fused_computation.87 | loop fusion | flops 4096 | bytes 1232 | tf_op jit(solution)/shard_map/mul | solution.py:28
  4.7 0.7 %multiply_select_fusion.7.table_ref = f32[16,128]{1,0:T(8,128)} fusion(f32[16]{0:T(128)S(1)} %get-tuple-element.59, s32[128]{0:T(128)S(1)} %get-tuple-element.50, s32[16]{0:T(128)S(1)} %add_select_fusion.10, pred[16]{0:T(512)(128)(4,1)S(1)} %fusion.39, pred[128]{0:T(512)(128)(4,1)S(1)} %broadcast_in_dim.118), kind=kLoop, calls=%fused_computation.88 | loop fusion | flops 34816 | bytes 8976 | tf_op jit(solution)/shard_map/jit(_where)/select_n | solution.py:615
  6.1 1.7 %shard_map.123 = (f32[16,4096]{1,0:T(8,128)S(1)}, f32[6,32,128]{2,1,0:T(8,128)S(1)}, f32[8,4096]{1,0:T(8,128)S(1)}, f32[32,4352]{1,0:T(8,128)S(1)}) custom-call(f32[16,4096]{1,0:T(8,128)S(1)} %get-tuple-element.25.v_ref, f32[16,4096]{1,0:T(8,128)S(1)} %get-tuple-element.26.sv_ref, f32[4,4096]{1,0:T(4,128)S(1)} %get-tuple-element.27.fw_ref, ...), custom_call_target="tpu_custom_call" | custom-call | tf_op jit(solution)/shard_map/pallas_call | solution.py:486
  10.1 2.5 %collective-permute-start.12 = (f32[32,128]{1,0:T(8,128)S(1)}, f32[32,128]{1,0:T(8,128)S(1)}, u32[]{:S(2)}, u32[]{:S(2)}) collective-permute-start(f32[32,128]{1,0:T(8,128)S(1)} %get-tuple-element.54), channel_id=1, source_target_pairs={{0,2},{2,4},{4,6},{6,8},{8,10},{10,12},{12,14},{14,0},{1,3},{3,5},... | collective-permute-start | bytes 49160 | tf_op jit(solution)/shard_map/ppermute | solution.py:651
  12.6 3.0 %collective-permute-start.13 = (f32[32,128]{1,0:T(8,128)S(1)}, f32[32,128]{1,0:T(8,128)S(1)}, u32[]{:S(2)}, u32[]{:S(2)}) collective-permute-start(f32[32,128]{1,0:T(8,128)S(1)} %get-tuple-element.53), channel_id=1, source_target_pairs={{2,0},{4,2},{6,4},{8,6},{10,8},{12,10},{14,12},{0,14},{3,1},{5,3},... | collective-permute-start | bytes 49160 | tf_op jit(solution)/shard_map/ppermute | solution.py:651
  16.2 1.2 %collective-permute-done.12 = f32[32,128]{1,0:T(8,128)S(1)} collective-permute-done((f32[32,128]{1,0:T(8,128)S(1)}, f32[32,128]{1,0:T(8,128)S(1)}, u32[]{:S(2)}, u32[]{:S(2)}) %collective-permute-start.12) | collective-permute-done | bytes 16416 | tf_op jit(solution)/shard_map/ppermute | solution.py:651
  18.1 1.4 %collective-permute-start.14 = (f32[2,32,128]{2,1,0:T(8,128)}, f32[2,32,128]{2,1,0:T(8,128)}, u32[]{:S(2)}, u32[]{:S(2)}) collective-permute-start(f32[2,32,128]{2,1,0:T(8,128)} %pad_maximum_fusion.1), channel_id=1, source_target_pairs={{0,2},{2,0},{4,6},{6,4},{8,10},{10,8},{12,14},{14,12},{1,3},{3,1},... | collective-permute-start | bytes 98312 | tf_op jit(solution)/shard_map/ppermute | solution.py:38
  20.8 3.6 %shard_map.125 = (s32[32,128]{1,0:T(8,128)S(1)}, bf16[16,4,2,128,128]{4,3,2,1,0:T(8,128)(2,1)S(1)}, bf16[16,2,2,128,128]{4,3,2,1,0:T(8,128)(2,1)S(1)}, bf16[16,1...) custom-call(s32[8,128]{1,0:T(8,128)S(1)} %copy-done.17, f32[16,4,128,128]{3,2,1,0:T(8,128)} %m1_hbm.1, ...), custom_call_target="tpu_custom_call" | custom-call | tf_op jit(solution)/shard_map/pallas_call | solution.py:486
  24.5 1.6 %collective-permute-start.1 = (f32[56,256]{1,0:T(8,128)S(1)}, f32[56,256]{1,0:T(8,128)S(1)}, u32[]{:S(2)}, u32[]{:S(2)}) collective-permute-start(f32[56,256]{1,0:T(8,128)S(1)} %copy-done.14), channel_id=1, source_target_pairs={{0,4},{2,6},{4,0},{6,2},{8,12},{10,14},{12,8},{14,10},{1,5},{3,7},... | collective-permute-start | bytes 172040 | tf_op jit(solution)/shard_map/ppermute | solution.py:38
  26.1 2.9 %collective-permute-start.2 = (f32[56,256]{1,0:T(8,128)S(1)}, f32[56,256]{1,0:T(8,128)S(1)}, u32[]{:S(2)}, u32[]{:S(2)}) collective-permute-start(f32[56,256]{1,0:T(8,128)S(1)} %copy-done.14), channel_id=1, source_target_pairs={{0,8},{2,10},{4,12},{6,14},{8,0},{10,2},{12,4},{14,6},{1,9},{3,11}... | collective-permute-start | bytes 172040 | tf_op jit(solution)/shard_map/ppermute | solution.py:38
  29.6 0.8 %fusion.30 = (f32[1,32,128]{2,1,0:T(8,128)S(1)}, f32[1,32,128]{2,1,0:T(8,128)S(1)}) fusion(f32[32,128]{1,0:T(8,128)S(1)} %copy-done.21, f32[2,32,128]{2,1,0:T(8,128)} %collective-permute-done.14, pred[]{:T(512)S(6)} %eq.102, f32[32,128]{1,0:T(8,128)S(1)} %get-tuple-element.29.diag_ref, f32[32,128]{1,0:T(8,128)S(1)} %copy-done.23), kind=kLoop, calls=%fused_computation.90 | loop fusion | flops 86016 | bytes 114689 | tf_op jit(solution)/shard_map/stack | solution.py:518
  30.5 1.4 %collective-permute-done.2 = f32[56,256]{1,0:T(8,128)S(1)} collective-permute-done((f32[56,256]{1,0:T(8,128)S(1)}, f32[56,256]{1,0:T(8,128)S(1)}, u32[]{:S(2)}, u32[]{:S(2)}) %collective-permute-start.2) | collective-permute-done | bytes 57376 | tf_op jit(solution)/shard_map/ppermute | solution.py:38
  31.9 3.0 %collective-permute-done.3 = f32[56,256]{1,0:T(8,128)S(1)} collective-permute-done((f32[56,256]{1,0:T(8,128)S(1)}, f32[56,256]{1,0:T(8,128)S(1)}, u32[]{:S(2)}, u32[]{:S(2)}) %collective-permute-start.3) | collective-permute-done | bytes 57376 | tf_op jit(solution)/shard_map/ppermute | solution.py:38
  35.5 0.8 %fusion.13 = (f32[32,128]{1,0:T(8,128)S(1)}, f32[32,128]{1,0:T(8,128)S(1)}) fusion(f32[2,32,128]{2,1,0:T(8,128)S(1)} %collective-permute-done.15, pred[]{:T(512)S(6)} %eq.101, f32[32,128]{1,0:T(8,128)S(1)} %copy-done.21, f32[2,32,128]{2,1,0:T(8,128)} %collective-permute-done.14, pred[]{:T(512)S(6)} %eq.102, f32[32,128]{1,0:T(8,128)S(1)} %get-tuple-element.29.diag_ref, ...), kind=kLoop, calls=%fused_computation.47 | loop fusion | flops 131072 | bytes 147458 | tf_op jit(solution)/shard_map/jit(_where)/select_n | solution.py:525
  36.9 1.0 %collective-permute-start.16 = (f32[2,32,128]{2,1,0:T(8,128)}, f32[2,32,128]{2,1,0:T(8,128)}, u32[]{:S(2)}, u32[]{:S(2)}) collective-permute-start(f32[2,32,128]{2,1,0:T(8,128)} %pad_maximum_fusion.3), channel_id=1, source_target_pairs={{0,8},{2,10},{4,12},{6,14},{8,0},{10,2},{12,4},{14,6},{1,9},{3,11}... | collective-permute-start | bytes 98312 | tf_op jit(solution)/shard_map/ppermute | solution.py:38
  37.9 2.6 %collective-permute-done.5.recv_ref = f32[168,256]{1,0:T(8,128)S(1)} collective-permute-done((f32[168,256]{1,0:T(8,128)S(1)}, f32[168,256]{1,0:T(8,128)S(1)}, u32[]{:S(2)}, u32[]{:S(2)}) %collective-permute-start.5) | collective-permute-done | bytes 172064 | tf_op jit(solution)/shard_map/ppermute | solution.py:38
  40.7 3.1 %shard_map.126 = (f32[16,128]{1,0:T(8,128)}, f32[16,8,128]{2,1,0:T(8,128)S(1)}) custom-call(s32[1]{0:T(128)} %bitcast.me_ref, f32[56,256]{1,0:T(8,128)S(1)} %copy-done.14, f32[168,256]{1,0:T(8,128)S(1)} %constant_dynamic-update-slice_fusion.mine_ref, f32[56,256]{1,0:T(8,128)S(1)} %collective-permute-done.4.beside_ref, ...), custom_call_target="tpu_custom_call" | custom-call | tf_op jit(solution)/shard_map/pallas_call | solution.py:486
  44.5 0.7 %multiply_select_fusion.6.table_ref = f32[24,128]{1,0:T(8,128)} fusion(f32[128]{0:T(128)S(1)} %copy-done.40, s32[24]{0:T(128)S(1)} %copy-done.41, s32[128]{0:T(128)S(1)} %copy-done.39, pred[128]{0:T(512)(128)(4,1)S(1)} %copy-done.35, pred[128]{0:T(512)(128)(4,1)S(1)} %copy-done.37), kind=kLoop, calls=%fused_computation.76 | loop fusion | flops 52224 | bytes 13664 | tf_op jit(solution)/shard_map/jit(_where)/select_n | solution.py:626
  45.3 0.7 %collective-permute-done.6.other_ref = f32[16,128]{1,0:T(8,128)} collective-permute-done((f32[16,128]{1,0:T(8,128)}, f32[16,128]{1,0:T(8,128)}, u32[]{:S(2)}, u32[]{:S(2)}) %collective-permute-start.6) | collective-permute-done | bytes 8224 | tf_op jit(solution)/shard_map/ppermute | solution.py:38
  46.0 2.2 %copy-done.1 = bf16[16,4,2,128,128]{4,3,2,1,0:T(8,128)(2,1)S(1)} copy-done((bf16[16,4,2,128,128]{4,3,2,1,0:T(8,128)(2,1)S(1)}, bf16[16,4,2,128,128]{4,3,2,1,0:T(8,128)(2,1)}, u32[]{:S(2)}) %copy-start.1) | copy-done | bytes 4194328
  48.2 1.2 %copy-done.7 = bf16[16,1,2,128,128]{4,3,2,1,0:T(8,128)(2,1)S(1)} copy-done((bf16[16,1,2,128,128]{4,3,2,1,0:T(8,128)(2,1)S(1)}, bf16[16,1,2,128,128]{4,3,2,1,0:T(8,128)(2,1)}, u32[]{:S(2)}) %copy-start.7) | copy-done | bytes 1048600
  49.4 0.8 %copy-done.10 = f32[16,8,128]{2,1,0:T(8,128)S(1)} copy-done((f32[16,8,128]{2,1,0:T(8,128)S(1)}, f32[16,8,128]{2,1,0:T(8,128)}, u32[]{:S(2)}) %copy-start.10) | copy-done | bytes 65560
  50.3 2.7 %shard_map.127 = f32[4,16,128]{2,1,0:T(8,128)S(1)} custom-call(f32[16,128]{1,0:T(8,128)} %get-tuple-element.40.s3_ref, f32[16,128]{1,0:T(8,128)} %collective-permute-done.6.other_ref, f32[16,8,128]{2,1,0:T(8,128)S(1)} %copy-done.10, bf16[16,4,2,128,128]{4,3,2,1,0:T(8,128)(2,1)S(1)} %copy-done.1, bf16[16,2,2,128,128]{4,3,2,1,0:T(8,128)(2,1)S(1)} %get-tuple-element.38.m2, ...), custom_call_target="tpu_custom_call" | custom-call | tf_op jit(solution)/shard_map/pallas_call | solution.py:486
  53.0 0.8 %fusion.4 = (f32[1,32,128]{2,1,0:T(8,128)S(1)}, f32[1,32,128]{2,1,0:T(8,128)S(1)}) fusion(f32[32,128]{1,0:T(8,128)S(1)} %copy-done.25, f32[2,32,128]{2,1,0:T(8,128)} %collective-permute-done.16, f32[2,32,128]{2,1,0:T(8,128)} %collective-permute-done.14, f32[2,32,128]{2,1,0:T(8,128)S(1)} %copy-done.33, pred[]{:T(512)S(6)} %eq.105, pred[]{:T(512)S(6)} %eq.104, ...), kind=kLoop, calls=%fused_computation.20 | loop fusion | flops 245760 | bytes 180233 | tf_op jit(solution)/shard_map/stack | solution.py:662
  53.9 1.3 %collective-permute-start.8 = (f32[64,128]{1,0:T(8,128)S(1)}, f32[64,128]{1,0:T(8,128)S(1)}, u32[]{:S(2)}, u32[]{:S(2)}) collective-permute-start(f32[64,128]{1,0:T(8,128)S(1)} %bitcast.83), channel_id=1, source_target_pairs={{0,8},{2,10},{4,12},{6,14},{8,0},{10,2},{12,4},{14,6},{1,9},{3,11}... | collective-permute-start | bytes 98312 | tf_op jit(solution)/shard_map/ppermute | solution.py:38
  55.2 3.1 %collective-permute-start.9 = (f32[64,128]{1,0:T(8,128)S(1)}, f32[64,128]{1,0:T(8,128)S(1)}, u32[]{:S(2)}, u32[]{:S(2)}) collective-permute-start(f32[64,128]{1,0:T(8,128)S(1)} %bitcast.84), channel_id=1, source_target_pairs={{0,12},{2,14},{4,8},{6,10},{8,4},{10,6},{12,0},{14,2},{1,13},{3,15... | collective-permute-start | bytes 98312 | tf_op jit(solution)/shard_map/ppermute | solution.py:38
  58.8 2.1 %collective-permute-done.9 = f32[64,128]{1,0:T(8,128)S(1)} collective-permute-done((f32[64,128]{1,0:T(8,128)S(1)}, f32[64,128]{1,0:T(8,128)S(1)}, u32[]{:S(2)}, u32[]{:S(2)}) %collective-permute-start.9) | collective-permute-done | bytes 32800 | tf_op jit(solution)/shard_map/ppermute | solution.py:38
  61.2 1.3 %collective-permute-done.10.beside_ref = f32[64,128]{1,0:T(8,128)S(1)} collective-permute-done((f32[64,128]{1,0:T(8,128)S(1)}, f32[64,128]{1,0:T(8,128)S(1)}, u32[]{:S(2)}, u32[]{:S(2)}) %collective-permute-start.10) | collective-permute-done | bytes 32800 | tf_op jit(solution)/shard_map/ppermute | solution.py:38
  62.4 3.1 %collective-permute-done.11.recv_ref = f32[192,128]{1,0:T(8,128)S(1)} collective-permute-done((f32[192,128]{1,0:T(8,128)S(1)}, f32[192,128]{1,0:T(8,128)S(1)}, u32[]{:S(2)}, u32[]{:S(2)}) %collective-permute-start.11) | collective-permute-done | bytes 98336 | tf_op jit(solution)/shard_map/ppermute | solution.py:38
  65.8 1.1 %shard_map.128.ext_in = f32[32,4352]{1,0:T(8,128)S(1)} custom-call(f32[64,128]{1,0:T(8,128)S(1)} %bitcast.87, f32[192,128]{1,0:T(8,128)S(1)} %constant_dynamic-update-slice_fusion.3.mine_ref, f32[64,128]{1,0:T(8,128)S(1)} %collective-permute-done.10.beside_ref, f32[192,128]{1,0:T(8,128)S(1)} %collective-permute-done.11.recv_ref, f32[24,128]{1,0:T(8,128)S(1)} %copy-done.8, ...), custom_call_target="tpu_custom_call" | custom-call | tf_op jit(solution)/shard_map/pallas_call | solution.py:486
  67.0 2.3 %shard_map.130 = (f32[16,4096]{1,0:T(8,128)}, f32[16,4096]{1,0:T(8,128)}) custom-call(f32[32,4352]{1,0:T(8,128)S(1)} %shard_map.128.ext_in, f32[16,4096]{1,0:T(8,128)S(1)} %copy-done.3, f32[16,128]{1,0:T(8,128)S(1)} %collective-permute-done.17.halo_ref, f32[16,4096]{1,0:T(8,128)S(1)} %get-tuple-element.26.sv_ref, f32[4,4096]{1,0:T(4,128)S(1)} %get-tuple-element.27.fw_ref, ...), custom_call_target="tpu_custom_call" | custom-call | tf_op jit(solution)/shard_map/pallas_call | solution.py:486
  (137 shorter events, 11.3 us)
Async XLA Ops:
  1.7 18.3 %copy-start.2 = (f32[16,4096]{1,0:T(8,128)}, f32[16,4096]{1,0:T(8,128)S(1)}, u32[]{:S(2)}) copy-start(f32[16,4096]{1,0:T(8,128)S(1)} %get-tuple-element.25.v_ref) | copy-start | bytes 786436
  1.7 18.3 %copy-start.16 = (s32[8,128]{1,0:T(8,128)}, s32[8,128]{1,0:T(8,128)S(1)}, u32[]{:S(2)}) copy-start(s32[8,128]{1,0:T(8,128)S(1)} %get-tuple-element.34.iface_ref) | copy-start | bytes 12292
  1.8 6.0 %collective-permute-start = (f32[16,128]{1,0:T(8,128)S(1)}, f32[16,128]{1,0:T(8,128)S(1)}, u32[]{:S(2)}, u32[]{:S(2)}) collective-permute-start(f32[16,128]{1,0:T(8,128)S(1)} %get-tuple-element.24), channel_id=1, source_target_pairs={{0,1},{1,0},{2,3},{3,2},{4,5},{5,4},{6,7},{7,6},{8,9},{9,8},{10,11... | collective-permute-start | bytes 24584 | tf_op jit(solution)/shard_map/ppermute | solution.py:38
  10.1 7.3 %collective-permute-start.12 = (f32[32,128]{1,0:T(8,128)S(1)}, f32[32,128]{1,0:T(8,128)S(1)}, u32[]{:S(2)}, u32[]{:S(2)}) collective-permute-start(f32[32,128]{1,0:T(8,128)S(1)} %get-tuple-element.54), channel_id=1, source_target_pairs={{0,2},{2,4},{4,6},{6,8},{8,10},{10,12},{12,14},{14,0},{1,3},{3,5},... | collective-permute-start | bytes 49160 | tf_op jit(solution)/shard_map/ppermute | solution.py:651
  12.6 4.8 %collective-permute-start.13 = (f32[32,128]{1,0:T(8,128)S(1)}, f32[32,128]{1,0:T(8,128)S(1)}, u32[]{:S(2)}, u32[]{:S(2)}) collective-permute-start(f32[32,128]{1,0:T(8,128)S(1)} %get-tuple-element.53), channel_id=1, source_target_pairs={{2,0},{4,2},{6,4},{8,6},{10,8},{12,10},{14,12},{0,14},{3,1},{5,3},... | collective-permute-start | bytes 49160 | tf_op jit(solution)/shard_map/ppermute | solution.py:651
  18.1 11.5 %collective-permute-start.14 = (f32[2,32,128]{2,1,0:T(8,128)}, f32[2,32,128]{2,1,0:T(8,128)}, u32[]{:S(2)}, u32[]{:S(2)}) collective-permute-start(f32[2,32,128]{2,1,0:T(8,128)} %pad_maximum_fusion.1), channel_id=1, source_target_pairs={{0,2},{2,0},{4,6},{6,4},{8,10},{10,8},{12,14},{14,12},{1,3},{3,1},... | collective-permute-start | bytes 98312 | tf_op jit(solution)/shard_map/ppermute | solution.py:38
  20.8 19.7 %copy-start.34 = (f32[16,16]{1,0:T(8,128)S(1)}, f32[16,16]{1,0:T(8,128)}, u32[]{:S(2)}) copy-start(f32[16,16]{1,0:T(8,128)} %select_multiply_fusion) | copy-start | bytes 3076
  20.8 19.8 %copy-start.38 = (f32[16]{0:T(128)S(1)}, f32[16]{0:T(128)}, u32[]{:S(2)}) copy-start(f32[16]{0:T(128)} %get-tuple-element.60) | copy-start | bytes 196
  20.8 19.9 %copy-start.15 = (f32[16,128]{1,0:T(8,128)S(1)}, f32[16,128]{1,0:T(8,128)}, u32[]{:S(2)}) copy-start(f32[16,128]{1,0:T(8,128)} %multiply_select_fusion.7.table_ref) | copy-start | bytes 24580
  20.8 19.9 %copy-start.19 = (f32[8,128]{1,0:T(8,128)S(1)}, f32[8,128]{1,0:T(8,128)}, u32[]{:S(2)}) copy-start(f32[8,128]{1,0:T(8,128)} %copy-done.18) | copy-start | bytes 12292
  24.4 19.4 %copy-start = (bf16[16,4,2,128,128]{4,3,2,1,0:T(8,128)(2,1)}, bf16[16,4,2,128,128]{4,3,2,1,0:T(8,128)(2,1)S(1)}, u32[]{:S(2)}) copy-start(bf16[16,4,2,128,128]{4,3,2,1,0:T(8,128)(2,1)S(1)} %get-tuple-element.37.m1) | copy-start | bytes 12582916
  24.5 19.4 %copy-start.6 = (bf16[16,1,2,128,128]{4,3,2,1,0:T(8,128)(2,1)}, bf16[16,1,2,128,128]{4,3,2,1,0:T(8,128)(2,1)S(1)}, u32[]{:S(2)}) copy-start(bf16[16,1,2,128,128]{4,3,2,1,0:T(8,128)(2,1)S(1)} %get-tuple-element.42.root) | copy-start | bytes 3145732
  24.5 19.4 %copy-start.11 = (s32[32,128]{1,0:T(8,128)}, s32[32,128]{1,0:T(8,128)S(1)}, u32[]{:S(2)}) copy-start(s32[32,128]{1,0:T(8,128)S(1)} %get-tuple-element.45.inv_ref) | copy-start | bytes 49156
  24.5 6.0 %collective-permute-start.1 = (f32[56,256]{1,0:T(8,128)S(1)}, f32[56,256]{1,0:T(8,128)S(1)}, u32[]{:S(2)}, u32[]{:S(2)}) collective-permute-start(f32[56,256]{1,0:T(8,128)S(1)} %copy-done.14), channel_id=1, source_target_pairs={{0,4},{2,6},{4,0},{6,2},{8,12},{10,14},{12,8},{14,10},{1,5},{3,7},... | collective-permute-start | bytes 172040 | tf_op jit(solution)/shard_map/ppermute | solution.py:38
  26.1 5.8 %collective-permute-start.2 = (f32[56,256]{1,0:T(8,128)S(1)}, f32[56,256]{1,0:T(8,128)S(1)}, u32[]{:S(2)}, u32[]{:S(2)}) collective-permute-start(f32[56,256]{1,0:T(8,128)S(1)} %copy-done.14), channel_id=1, source_target_pairs={{0,8},{2,10},{4,12},{6,14},{8,0},{10,2},{12,4},{14,6},{1,9},{3,11}... | collective-permute-start | bytes 172040 | tf_op jit(solution)/shard_map/ppermute | solution.py:38
  29.0 6.0 %collective-permute-start.3 = (f32[56,256]{1,0:T(8,128)S(1)}, f32[56,256]{1,0:T(8,128)S(1)}, u32[]{:S(2)}, u32[]{:S(2)}) collective-permute-start(f32[56,256]{1,0:T(8,128)S(1)} %copy-done.14), channel_id=1, source_target_pairs={{0,12},{2,14},{4,8},{6,10},{8,4},{10,6},{12,0},{14,2},{1,13},{3,15... | collective-permute-start | bytes 172040 | tf_op jit(solution)/shard_map/ppermute | solution.py:38
  29.0 8.9 %collective-permute-start.4 = (f32[56,256]{1,0:T(8,128)S(1)}, f32[56,256]{1,0:T(8,128)S(1)}, u32[]{:S(2)}, u32[]{:S(2)}) collective-permute-start(f32[56,256]{1,0:T(8,128)S(1)} %copy-done.14), channel_id=1, source_target_pairs={{0,2},{2,0},{4,6},{6,4},{8,10},{10,8},{12,14},{14,12},{1,3},{3,1},... | collective-permute-start | bytes 172040 | tf_op jit(solution)/shard_map/ppermute | solution.py:38
  30.4 5.1 %collective-permute-start.15 = (f32[2,32,128]{2,1,0:T(8,128)S(1)}, f32[2,32,128]{2,1,0:T(8,128)S(1)}, u32[]{:S(2)}, u32[]{:S(2)}) collective-permute-start(f32[2,32,128]{2,1,0:T(8,128)S(1)} %pad_maximum_fusion.2), channel_id=1, source_target_pairs={{0,4},{2,6},{4,0},{6,2},{8,12},{10,14},{12,8},{14,10},{1,5},{3,7},... | collective-permute-start | bytes 98312 | tf_op jit(solution)/shard_map/ppermute | solution.py:38
  35.0 5.5 %collective-permute-start.5 = (f32[168,256]{1,0:T(8,128)S(1)}, f32[168,256]{1,0:T(8,128)S(1)}, u32[]{:S(2)}, u32[]{:S(2)}) collective-permute-start(f32[168,256]{1,0:T(8,128)S(1)} %constant_dynamic-update-slice_fusion.mine_ref), channel_id=1, source_target_pairs={{0,2},{2,0},{4,6},{6,4},{8,10},{10,8},{12,14},{14,12},{1,3},{3,1},... | collective-permute-start | bytes 516104 | tf_op jit(solution)/shard_map/ppermute | solution.py:38
  36.9 16.1 %collective-permute-start.16 = (f32[2,32,128]{2,1,0:T(8,128)}, f32[2,32,128]{2,1,0:T(8,128)}, u32[]{:S(2)}, u32[]{:S(2)}) collective-permute-start(f32[2,32,128]{2,1,0:T(8,128)} %pad_maximum_fusion.3), channel_id=1, source_target_pairs={{0,8},{2,10},{4,12},{6,14},{8,0},{10,2},{12,4},{14,6},{1,9},{3,11}... | collective-permute-start | bytes 98312 | tf_op jit(solution)/shard_map/ppermute | solution.py:38
  44.4 1.5 %collective-permute-start.6 = (f32[16,128]{1,0:T(8,128)}, f32[16,128]{1,0:T(8,128)}, u32[]{:S(2)}, u32[]{:S(2)}) collective-permute-start(f32[16,128]{1,0:T(8,128)} %get-tuple-element.40.s3_ref), channel_id=1, source_target_pairs={{0,1},{1,0},{2,3},{3,2},{4,5},{5,4},{6,7},{7,6},{8,9},{9,8},{10,11... | collective-permute-start | bytes 24584 | tf_op jit(solution)/shard_map/ppermute | solution.py:38
  50.2 10.9 %copy-start.29 = (f32[32,128]{1,0:T(8,128)S(1)}, f32[32,128]{1,0:T(8,128)}, u32[]{:S(2)}) copy-start(f32[32,128]{1,0:T(8,128)} %copy-done.28) | copy-start | bytes 49156
  50.2 15.3 %copy-start.5 = (f32[16,4096]{1,0:T(8,128)S(1)}, f32[16,4096]{1,0:T(8,128)}, u32[]{:S(2)}) copy-start(f32[16,4096]{1,0:T(8,128)} %copy-done.4) | copy-start | bytes 786436
  50.3 15.3 %copy-start.8 = (f32[24,128]{1,0:T(8,128)S(1)}, f32[24,128]{1,0:T(8,128)}, u32[]{:S(2)}) copy-start(f32[24,128]{1,0:T(8,128)} %multiply_select_fusion.6.table_ref) | copy-start | bytes 36868
  50.3 15.3 %copy-start.12 = (s32[32,128]{1,0:T(8,128)S(1)}, s32[32,128]{1,0:T(8,128)}, u32[]{:S(2)}) copy-start(s32[32,128]{1,0:T(8,128)} %copy-done.11) | copy-start | bytes 49156
  50.3 16.7 %copy-start.3 = (f32[16,4096]{1,0:T(8,128)S(1)}, f32[16,4096]{1,0:T(8,128)}, u32[]{:S(2)}) copy-start(f32[16,4096]{1,0:T(8,128)} %copy-done.2) | copy-start | bytes 786436
  52.9 5.7 %collective-permute-start.7 = (f32[64,128]{1,0:T(8,128)S(1)}, f32[64,128]{1,0:T(8,128)S(1)}, u32[]{:S(2)}, u32[]{:S(2)}) collective-permute-start(f32[64,128]{1,0:T(8,128)S(1)} %bitcast.82), channel_id=1, source_target_pairs={{0,4},{2,6},{4,0},{6,2},{8,12},{10,14},{12,8},{14,10},{1,5},{3,7},... | collective-permute-start | bytes 98312 | tf_op jit(solution)/shard_map/ppermute | solution.py:38
  53.9 4.9 %collective-permute-start.8 = (f32[64,128]{1,0:T(8,128)S(1)}, f32[64,128]{1,0:T(8,128)S(1)}, u32[]{:S(2)}, u32[]{:S(2)}) collective-permute-start(f32[64,128]{1,0:T(8,128)S(1)} %bitcast.83), channel_id=1, source_target_pairs={{0,8},{2,10},{4,12},{6,14},{8,0},{10,2},{12,4},{14,6},{1,9},{3,11}... | collective-permute-start | bytes 98312 | tf_op jit(solution)/shard_map/ppermute | solution.py:38
  55.2 5.7 %collective-permute-start.9 = (f32[64,128]{1,0:T(8,128)S(1)}, f32[64,128]{1,0:T(8,128)S(1)}, u32[]{:S(2)}, u32[]{:S(2)}) collective-permute-start(f32[64,128]{1,0:T(8,128)S(1)} %bitcast.84), channel_id=1, source_target_pairs={{0,12},{2,14},{4,8},{6,10},{8,4},{10,6},{12,0},{14,2},{1,13},{3,15... | collective-permute-start | bytes 98312 | tf_op jit(solution)/shard_map/ppermute | solution.py:38
  58.3 4.2 %collective-permute-start.10 = (f32[64,128]{1,0:T(8,128)S(1)}, f32[64,128]{1,0:T(8,128)S(1)}, u32[]{:S(2)}, u32[]{:S(2)}) collective-permute-start(f32[64,128]{1,0:T(8,128)S(1)} %bitcast.85), channel_id=1, source_target_pairs={{0,2},{2,0},{4,6},{6,4},{8,10},{10,8},{12,14},{14,12},{1,3},{3,1},... | collective-permute-start | bytes 98312 | tf_op jit(solution)/shard_map/ppermute | solution.py:38
  60.9 4.6 %collective-permute-start.11 = (f32[192,128]{1,0:T(8,128)S(1)}, f32[192,128]{1,0:T(8,128)S(1)}, u32[]{:S(2)}, u32[]{:S(2)}) collective-permute-start(f32[192,128]{1,0:T(8,128)S(1)} %constant_dynamic-update-slice_fusion.3.mine_ref), channel_id=1, source_target_pairs={{0,2},{2,0},{4,6},{6,4},{8,10},{10,8},{12,14},{14,12},{1,3},{3,1},... | collective-permute-start | bytes 294920 | tf_op jit(solution)/shard_map/ppermute | solution.py:38
  65.8 1.2 %collective-permute-start.17 = (f32[16,128]{1,0:T(8,128)S(1)}, f32[16,128]{1,0:T(8,128)S(1)}, u32[]{:S(2)}, u32[]{:S(2)}) collective-permute-start(f32[16,128]{1,0:T(8,128)S(1)} %shard_map.129), channel_id=1, source_target_pairs={{0,1},{1,0},{2,3},{3,2},{4,5},{5,4},{6,7},{7,6},{8,9},{9,8},{10,11... | collective-permute-start | bytes 24584 | tf_op jit(solution)/shard_map/ppermute | solution.py:38
  (28 other events, 135.9 us)
